TPU v7x, 128 devices: a whole 4x4x4 slice. The times are simulated.
128 devices in a mesh: dp: 16 (over x, y), bag: 8 (over z, core).
Axes of the slice: x: 4, y: 4, z: 4, core: 2. Of those that a mesh axis runs over, the one named last changes fastest.
Arguments:
- home_tokens: bfloat16 [16384, 3072], P('dp', 'bag'), may hold values from -6 to 6
- mod_weight: bfloat16 [2, 3072, 3072], P(None, None, 'bag'), may hold values from -0.109375 to 0.109375
- qkv_weight: bfloat16 [3, 3072, 3072], P(None, None, 'bag')
- norm_gain: float32 [2, 3072], P(None, 'bag'), may hold values from 0.5 to 8
- output_weight: bfloat16 [3072, 3072], P('bag'), may hold values from -0.109375 to 0.109375
- row_plan: int32 [16384], replicated, may hold values from 0 to 20479, as said below
- sample_lengths: int32 [16, 4], replicated, may hold values from 0 to 1280, as said below
- modality: int32 [16, 4], replicated, may hold values from 0 to 1
Outputs:
- block_output: bfloat16 [16384, 3072], P('dp', 'bag')
Inputs may be any that keep to these rules, and one draw needn't show every extreme that they name: `row_plan`: row r sits on home r // 1024; no two rows share a value; the rows of bag j fill exactly its slots 0 to sample_ends[j, 3] - 1; no home sends more than 128 rows to one bag, and some home sends exactly 128 rows to some bag. `sample_lengths`: row j lists the lengths of the samples of bag j in slot order, zeros allowed; each row sums to at most 1280, and some bag holds one sample of 1280 tokens.
All inputs are finite; a program needn't handle non-finite values.
Results may differ from a plain program's by a relative error of at most 0.013.
The roundings to bfloat16 on the way count: a program that leaves them out, or rounds other values in their place, can miss the bound.
Values may be sent and summed in bfloat16 or wider, within the bound.
A program may use at most 192 MiB of HBM per device.

v0:
```python
import jax
import jax.numpy as jnp
from jax import lax
from jax.sharding import PartitionSpec as P

HD = 64


epsilon = 1e-06


def head_norm(heads_in, gains):
    centre = jnp.mean(heads_in, axis=-1, keepdims=True)
    shifted = heads_in - centre
    spread = jnp.mean(shifted * shifted, axis=-1, keepdims=True)
    return shifted * lax.rsqrt(spread + epsilon) * gains


def body(
    home_tokens,
    mod_weight,
    qkv_weight,
    norm_gain,
    output_weight,
    row_plan,
    sample_lengths,
    modality,
):
    dev_count = lax.axis_size("dp")
    members = lax.axis_size("bag")
    my_home = lax.axis_index("dp")
    resident_rows, width_part = home_tokens.shape
    pack_size = resident_rows + resident_rows // 4
    total_rows = row_plan.shape[0]
    capacity = 2 * resident_rows // dev_count
    send_slots = capacity * dev_count
    full_width = width_part * members
    head_width = output_weight.shape[0]
    head_count = head_width // HD
    bag_ids = jnp.arange(dev_count, dtype=jnp.int32)
    sample_ends = jnp.cumsum(sample_lengths, axis=1)
    dest_bag = row_plan // pack_size
    dest_slot = row_plan % pack_size
    bag_match = dest_bag[:, None] == bag_ids[None, :]
    rows_per_resident = bag_match.astype(jnp.bfloat16).reshape(dev_count, resident_rows, dev_count)
    row_ids = jnp.arange(resident_rows, dtype=jnp.int32)
    lower_bound = (row_ids[:, None] > row_ids[None, :]).astype(jnp.bfloat16)
    preceding_rows = jnp.einsum(
        "mt,pta->pma", lower_bound, rows_per_resident, preferred_element_type=jnp.float32
    )
    position = (
        jnp.sum(preceding_rows * rows_per_resident.astype(jnp.float32), axis=2)
        .astype(jnp.int32)
        .reshape(total_rows)
    )
    home_of = jnp.arange(total_rows, dtype=jnp.int32) // resident_rows
    send_index = position * dev_count + dest_bag
    recv_index = jnp.where(dest_bag == my_home, position * dev_count + home_of, send_slots)
    slot_table = (
        jnp.full((send_slots,), pack_size, jnp.int32).at[recv_index].set(dest_slot, mode="drop")
    )
    slot_source = (
        jnp.full((pack_size,), send_slots, jnp.int32)
        .at[slot_table]
        .set(jnp.arange(send_slots, dtype=jnp.int32), mode="drop")
    )
    own_start = my_home * resident_rows
    own_hits = lax.dynamic_slice_in_dim(bag_match.astype(jnp.int32), own_start, resident_rows, 0)
    own_slot = lax.dynamic_slice_in_dim(dest_slot, own_start, resident_rows, 0)
    own_index = lax.dynamic_slice_in_dim(send_index, own_start, resident_rows, 0)
    row_ends = jnp.dot(own_hits, sample_ends)
    row_sample = jnp.sum((own_slot[:, None] >= row_ends).astype(jnp.int32), axis=1)
    sample_hits = (
        row_sample[:, None] == jnp.arange(sample_ends.shape[1], dtype=jnp.int32)[None, :]
    ).astype(jnp.int32)
    row_modality = jnp.sum(jnp.dot(own_hits, modality) * sample_hits, axis=1)
    is_first = (row_modality == 0)[:, None]
    pieces = lax.all_gather(home_tokens, "bag", axis=1, tiled=True)
    blank = jnp.zeros_like(pieces)
    first_part = jnp.where(is_first, pieces, blank)
    second_part = jnp.where(is_first, blank, pieces)
    running = jnp.dot(first_part, mod_weight[0], preferred_element_type=jnp.float32)
    projected = (
        running + jnp.dot(second_part, mod_weight[1], preferred_element_type=jnp.float32)
    ).astype(jnp.bfloat16)
    send_onehot = (jnp.arange(send_slots, dtype=jnp.int32)[:, None] == own_index[None, :]).astype(
        jnp.bfloat16
    )
    send_flat = jnp.dot(send_onehot, projected, preferred_element_type=jnp.float32).astype(
        jnp.bfloat16
    )
    outgoing_rows = send_flat.reshape(capacity, dev_count, width_part)
    copies = jnp.broadcast_to(
        outgoing_rows[:, :, None, :], (capacity, dev_count, members, width_part)
    )
    copies = copies.reshape(capacity, dev_count * members, width_part)
    arrived = lax.all_to_all(copies, ("dp", "bag"), split_axis=1, concat_axis=1, tiled=True)
    arrived = arrived.reshape(send_slots, full_width)
    packed = jnp.take(arrived, slot_source, axis=0, mode="fill", fill_value=0)
    stacked = jnp.einsum("pd,kdh->kph", packed, qkv_weight, preferred_element_type=jnp.float32)
    my_ends = jnp.sum(jnp.where((bag_ids == my_home)[:, None], sample_ends, 0), axis=0)
    slot_ids = jnp.arange(pack_size, dtype=jnp.int32)
    sample_ids = jnp.sum((slot_ids[:, None] >= my_ends[None, :]).astype(jnp.int32), axis=1)
    queries = head_norm(
        stacked[0].reshape(pack_size, head_count, HD), norm_gain[0].reshape(head_count, HD)
    ).astype(jnp.bfloat16)
    keys_normed = head_norm(
        stacked[1].reshape(pack_size, head_count, HD), norm_gain[1].reshape(head_count, HD)
    ).astype(jnp.bfloat16)
    values = stacked[2].astype(jnp.bfloat16).reshape(pack_size, head_count, HD)
    blocks = max(1, pack_size // 512)
    block_rows = pack_size // blocks

    def attend(block_index):
        offset = block_index * block_rows
        query_block = lax.dynamic_slice_in_dim(queries, offset, block_rows, 0)
        sample_block = lax.dynamic_slice_in_dim(sample_ids, offset, block_rows, 0)
        scores = jnp.einsum(
            "qhd,khd->hqk", query_block, keys_normed, preferred_element_type=jnp.float32
        ) * HD ** (-0.5)
        scores = jnp.where((sample_block[:, None] == sample_ids[None, :])[None], scores, -jnp.inf)
        row_max = jnp.max(scores, axis=2, keepdims=True)
        raised = jnp.exp(scores - row_max)
        weights_soft = (raised / jnp.sum(raised, axis=2, keepdims=True)).astype(jnp.bfloat16)
        return jnp.einsum(
            "hqk,khd->qhd", weights_soft, values, preferred_element_type=jnp.float32
        ).astype(jnp.bfloat16)

    attended = lax.map(attend, jnp.arange(blocks, dtype=jnp.int32)).reshape(pack_size, head_width)
    partial_value = jnp.dot(attended, output_weight, preferred_element_type=jnp.float32)
    partial_low = partial_value.astype(jnp.bfloat16)
    back_rows = jnp.take(partial_low, slot_table, axis=0, mode="fill", fill_value=0)
    back_rows = back_rows.reshape(capacity, dev_count * members, width_part)
    returned = lax.all_to_all(back_rows, ("dp", "bag"), split_axis=1, concat_axis=1, tiled=True)
    combined = jnp.sum(
        returned.reshape(capacity, dev_count, members, width_part).astype(jnp.float32), axis=2
    )
    combined = combined.reshape(send_slots, width_part)
    result = jnp.take(combined, own_index, axis=0)
    return result.astype(jnp.bfloat16)


def solution(mesh):
    in_specs = (
        P("dp", "bag"),
        P(None, None, "bag"),
        P(None, None, "bag"),
        P(None, "bag"),
        P("bag", None),
        P(),
        P(),
        P(),
    )
    out_specs = P("dp", "bag")
    return jax.shard_map(body, mesh=mesh, in_specs=in_specs, out_specs=out_specs, check_vma=False)
```

profile of v0, /device:TPU:38, one launch (start us, length us, event | category | flops | bytes accessed | tf_op | source)
XLA Modules:
  0.0 647.2 jit_solution(7662121125258490245)
XLA Ops:
  12.3 38.7 %all-gather.2.cloned.1.call-done = bf16[1024,3072]{1,0:T(8,128)(2,1)} async-done(((bf16[1024,384]{1,0:T(8,128)(2,1)}), bf16[1024,3072]{1,0:T(8,128)(2,1)}) %all-gather.2.cloned.1.call-update) | async-done | bytes 6291472 | tf_op jit(solution)/shard_map/all_gather | solution.py:78
  51.0 8.2 %fusion.32 = f32[1024,384]{1,0:T(8,128)} fusion(bf16[1024,3072]{1,0:T(8,128)(2,1)} %all-gather.2.cloned.1.call-done, pred[1024]{0:T(1024)(128)(4,1)S(1)} %broadcast_compare_fusion.1, bf16[2,3072,384]{2,1,0:T(8,128)(2,1)} %param.11), kind=kOutput, calls=%fused_computation.35 | convolution fusion | flops 2419064832 | bytes 10224640 | tf_op jit(solution)/shard_map/dot_general | solution.py:84
  59.2 10.7 %fusion.48 = bf16[2048,384]{1,0:T(8,128)(2,1)} fusion(s32[1024]{0:T(1024)S(1)} %get-tuple-element.60, f32[1024,384]{1,0:T(8,128)} %fusion.32, bf16[2,3072,384]{2,1,0:T(8,128)(2,1)} %param.11, bf16[1024,3072]{1,0:T(8,128)(2,1)} %all-gather.2.cloned.1.call-done, pred[1024]{0:T(1024)(128)(4,1)S(1)} %broadcast_compare_fusion.1), kind=kOutput, calls=%fused_computation.49 | convolution fusion | flops 4033347584 | bytes 11801600 | tf_op jit(solution)/shard_map/dot_general | solution.py:89
  69.9 3.0 copy.28
  72.9 8.0 %broadcast_in_dim.143 = bf16[128,16,8,384]{3,0,2,1:T(8,128)(2,1)} broadcast(bf16[128,16,384]{2,0,1:T(8,128)(2,1)} %copy.28), dimensions={0,1,3} | broadcast | bytes 14155776 | tf_op jit(solution)/shard_map/broadcast_in_dim | solution.py:93
  80.9 9.6 %all-to-all-start = ((bf16[128,128,384]{2,0,1:T(8,128)(2,1)}), bf16[128,128,384]{2,0,1:T(8,128)(2,1)}, u32[]{:S(2)}, u32[]{:S(2)}) async-start(bf16[128,128,384]{2,0,1:T(8,128)(2,1)} %bitcast.76), calls=%async_computation | async-start | bytes 25165824 | tf_op jit(solution)/shard_map/all_to_all | solution.py:97
  90.7 60.3 %scatter_custom_fusion = s32[2048]{0:T(1024)S(1)} fusion(s32[16384]{0:T(1024)S(1)} %get-tuple-element.64, s32[16384]{0:T(1024)S(1)} %get-tuple-element.65, s32[]{:T(128)} %constant.110.clone.1), kind=kCustom, calls=%fused_computation.109 | custom fusion | bytes 8196 | tf_op jit(solution)/shard_map/scatter | solution.py:60
  151.8 8.0 %scatter_custom_fusion.1 = s32[1280]{0:T(1024)S(1)} fusion(s32[2048]{0:T(1024)S(1)} %get-tuple-element.67, s32[2048]{0:T(1024)S(1)} %iota.47, s32[]{:T(128)} %constant.119.clone.1), kind=kCustom, calls=%fused_computation.107 | custom fusion | bytes 5124 | tf_op jit(solution)/shard_map/scatter | solution.py:65
  160.7 97.0 %all-to-all-done = bf16[128,128,384]{2,0,1:T(8,128)(2,1)} async-done(((bf16[128,128,384]{2,0,1:T(8,128)(2,1)}), bf16[128,128,384]{2,0,1:T(8,128)(2,1)}, u32[]{:S(2)}, u32[]{:S(2)}) %all-to-all-start) | async-done | bytes 12582944 | tf_op jit(solution)/shard_map/all_to_all | solution.py:97
  257.7 15.0 %copy.29 = bf16[128,128,384]{2,1,0:T(8,128)(2,1)} copy(bf16[128,128,384]{2,0,1:T(8,128)(2,1)} %all-to-all-done) | data formatting | bytes 25165824 | tf_op jit(solution)/shard_map/all_to_all | solution.py:97
  272.7 19.5 %reshape.138 = bf16[2048,3072]{1,0:T(8,128)(2,1)} reshape(bf16[128,128,384]{2,1,0:T(8,128)(2,1)} %copy.29) | data formatting | bytes 25165824 | tf_op jit(solution)/shard_map/reshape | solution.py:98
  292.2 21.3 %gather_fusion = bf16[1280,3072]{1,0:T(8,128)(2,1)} fusion(bf16[2048,3072]{1,0:T(8,128)(2,1)} %reshape.138, s32[2048]{0:T(1024)S(1)} %pad_clamp_fusion), kind=kCustom, calls=%fused_computation | custom fusion | bytes 15733760 | tf_op jit(solution)/shard_map/jit(_take)/gather | solution.py:99
  313.4 14.6 %fusion.38 = f32[3,1280,384]{1,2,0:T(8,128)S(1)} fusion(bf16[3,3072,384]{2,1,0:T(8,128)(2,1)} %param.12, bf16[1280,3072]{1,0:T(8,128)(2,1)} %gather_fusion, pred[1280]{0:T(1024)(128)(4,1)S(1)} %compare_and_fusion), kind=kOutput, calls=%fused_computation.41 | convolution fusion | flops 9063628800 | bytes 20841728 | tf_op jit(solution)/shard_map/pd,kdh->kph/dot_general | solution.py:100
  328.0 2.1 fusion.94
  332.9 1.8 multiply_reduce_fusion.1
  336.5 1.8 multiply_reduce_fusion
  338.3 4.1 multiply_convert_fusion
  342.4 39.9 %while.10 = (s32[]{:T(128)}, bf16[2,640,6,64]{1,3,2,0:T(8,128)(2,1)}, s32[2]{0:T(128)S(1)}, s32[1280]{0:T(1024)S(1)}, bf16[1280,6,64]{0,2,1:T(8,128)(2,1)}, /*in...) while((s32[]{:T(128)}, ...), condition=%wide.region_15.16_spmd, body=%wide.region_12.15_spmd.sunk | while | flops 1932744960 | bytes 6925491 | solution.py:129
  344.5 7.8 %exponential_reduce_fusion.2 = f32[6,640]{1,0:T(8,128)S(1)} fusion(bf16[1280,6,64]{0,2,1:T(8,128)(2,1)} %get-tuple-element.140, pred[640,1280]{1,0:T(8,128)(4,1)S(1)} %broadcast_compare_fusion.3, bf16[1280,6,64]{0,2,1:T(8,128)(2,1)} %get-tuple-element.139, s32[]{:T(128)S(6)} %select_n.151), kind=kOutput, calls=%fused_computation.9.clone.1 | convolution fusion | flops 648807680 | bytes 2309124 | tf_op jit(solution)/shard_map/while/body/eval_jaxpr/sub | solution.py:123
  352.3 10.0 %fusion.114 = bf16[2,640,6,64]{1,3,2,0:T(8,128)(2,1)} fusion(bf16[2,640,6,64]{1,3,2,0:T(8,128)(2,1)} %get-tuple-element.125, s32[]{:T(128)} %get-tuple-element.124, bf16[1280,6,64]{0,2,1:T(8,128)(2,1)} %get-tuple-element.141, f32[6,640]{1,0:T(8,128)S(1)} %exponential_reduce_fusion.2, bf16[1280,6,64]{0,2,1:T(8,128)(2,1)} %get-tuple-element.140, ...), kind=kOutput, calls=%fused_computation.14.clone.1 | convolution fusion | flops 1283118080 | bytes 3784196 | tf_op jit(solution)/shard_map/while/body/eval_jaxpr/hqk,khd->qhd/dot_general | solution.py:125
  364.3 7.8 %exponential_reduce_fusion.2 = f32[6,640]{1,0:T(8,128)S(1)} fusion(bf16[1280,6,64]{0,2,1:T(8,128)(2,1)} %get-tuple-element.140, pred[640,1280]{1,0:T(8,128)(4,1)S(1)} %broadcast_compare_fusion.3, bf16[1280,6,64]{0,2,1:T(8,128)(2,1)} %get-tuple-element.139, s32[]{:T(128)S(6)} %select_n.151), kind=kOutput, calls=%fused_computation.9.clone.1 | convolution fusion | flops 648807680 | bytes 2309124 | tf_op jit(solution)/shard_map/while/body/eval_jaxpr/sub | solution.py:123
  372.1 10.0 %fusion.114 = bf16[2,640,6,64]{1,3,2,0:T(8,128)(2,1)} fusion(bf16[2,640,6,64]{1,3,2,0:T(8,128)(2,1)} %get-tuple-element.125, s32[]{:T(128)} %get-tuple-element.124, bf16[1280,6,64]{0,2,1:T(8,128)(2,1)} %get-tuple-element.141, f32[6,640]{1,0:T(8,128)S(1)} %exponential_reduce_fusion.2, bf16[1280,6,64]{0,2,1:T(8,128)(2,1)} %get-tuple-element.140, ...), kind=kOutput, calls=%fused_computation.14.clone.1 | convolution fusion | flops 1283118080 | bytes 3784196 | tf_op jit(solution)/shard_map/while/body/eval_jaxpr/hqk,khd->qhd/dot_general | solution.py:125
  382.3 2.2 copy.31
  384.6 6.5 convolution_convert_fusion
  391.1 27.2 %gather_fusion.1 = bf16[2048,3072]{1,0:T(8,128)(2,1)} fusion(bf16[1280,3072]{1,0:T(8,128)(2,1)} %convolution_convert_fusion, s32[2048]{0:T(1024)S(1)} %copy-done.2), kind=kCustom, calls=%fused_computation.1 | custom fusion | bytes 25174016 | tf_op jit(solution)/shard_map/jit(_take)/gather | solution.py:132
  418.3 19.5 %gather.16 = bf16[128,128,384]{2,1,0:T(8,128)(2,1)} reshape(bf16[2048,3072]{1,0:T(8,128)(2,1)} %gather_fusion.1) | data formatting | bytes 25165824 | tf_op jit(solution)/shard_map/jit(_take)/gather | solution.py:132
  437.8 11.0 %copy_select_fusion = bf16[128,128,384]{2,0,1:T(8,128)(2,1)} fusion(bf16[128,128,384]{2,1,0:T(8,128)(2,1)} %gather.16, pred[128,128]{0,1:T(8,128)(4,1)S(1)} %copy-done.1), kind=kLoop, calls=%fused_computation.27 | loop fusion | flops 6291456 | bytes 25182208 | tf_op jit(solution)/shard_map/jit(_take)/select_n | solution.py:132
  448.8 5.6 all-to-all-start.1
  454.4 167.2 %all-to-all-done.1 = bf16[128,128,384]{2,0,1:T(8,128)(2,1)} async-done(((bf16[128,128,384]{2,0,1:T(8,128)(2,1)}), bf16[128,128,384]{2,0,1:T(8,128)(2,1)}, u32[]{:S(2)}, u32[]{:S(2)}) %all-to-all-start.1) | async-done | bytes 12582944 | tf_op jit(solution)/shard_map/all_to_all | solution.py:134
  621.6 8.3 %convert_reduce_fusion = bf16[128,16,384]{2,0,1:T(8,128)(2,1)} fusion(bf16[128,128,384]{2,0,1:T(8,128)(2,1)} %all-to-all-done.1), kind=kLoop, calls=%fused_computation.26 | loop fusion | flops 11796480 | bytes 14155776 | tf_op jit(solution)/shard_map/reduce_sum | solution.py:135
  629.9 3.5 copy.33
  633.3 5.4 gather_fusion.2
  (61 shorter events, 15.9 us)
Async XLA Ops:
  6.5 378.1 %copy-start = (bf16[384,3072]{1,0:T(8,128)(2,1)S(1)}, bf16[384,3072]{1,0:T(8,128)(2,1)}, u32[]{:S(2)}) copy-start(bf16[384,3072]{1,0:T(8,128)(2,1)} %param.14) | copy-start | bytes 7077892
  6.5 44.4 %all-gather.2.cloned.1.call-start = ((), (), s32[]{:S(2)}) async-start(), calls=%async_computation.2 | async-start | bytes 7077888 | tf_op jit(solution)/shard_map/all_gather | solution.py:78
  11.3 47.9 %copy-start.3 = (s32[1024]{0:T(1024)}, s32[1024]{0:T(1024)S(1)}, u32[]{:S(2)}) copy-start(s32[1024]{0:T(1024)S(1)} %get-tuple-element.60) | copy-start | bytes 12292
  80.9 9.6 %copy-start.6 = (f32[2,384]{1,0:T(2,128)S(1)}, f32[2,384]{1,0:T(2,128)}, u32[]{:S(2)}) copy-start(f32[2,384]{1,0:T(2,128)} %param.13) | copy-start | bytes 9220
  80.9 176.8 %all-to-all-start = ((bf16[128,128,384]{2,0,1:T(8,128)(2,1)}), bf16[128,128,384]{2,0,1:T(8,128)(2,1)}, u32[]{:S(2)}, u32[]{:S(2)}) async-start(bf16[128,128,384]{2,0,1:T(8,128)(2,1)} %bitcast.76), calls=%async_computation | async-start | bytes 25165824 | tf_op jit(solution)/shard_map/all_to_all | solution.py:97
  384.6 6.5 %copy-start.2 = (s32[2048]{0:T(1024)S(1)}, s32[2048]{0:T(1024)}, u32[]{:S(2)}) copy-start(s32[2048]{0:T(1024)} %get-tuple-element.66) | copy-start | bytes 24580
  418.3 19.5 %copy-start.1 = (pred[128,128]{0,1:T(8,128)(4,1)S(1)}, pred[128,128]{0,1:T(8,128)(4,1)}, u32[]{:S(2)}) copy-start(pred[128,128]{0,1:T(8,128)(4,1)} %broadcast_bitcast_fusion) | copy-start | bytes 49156
  448.8 5.6 copy-start.4
  448.8 172.8 %all-to-all-start.1 = ((bf16[128,128,384]{2,0,1:T(8,128)(2,1)}), bf16[128,128,384]{2,0,1:T(8,128)(2,1)}, u32[]{:S(2)}, u32[]{:S(2)}) async-start(bf16[128,128,384]{2,0,1:T(8,128)(2,1)} %copy_select_fusion), calls=%async_computation.1 | async-start | bytes 25165824 | tf_op jit(solution)/shard_map/all_to_all | solution.py:134
  629.9 8.9 %copy-start.5 = (pred[1024]{0:T(1024)(128)(4,1)S(1)}, pred[1024]{0:T(1024)(128)(4,1)}, u32[]{:S(2)}) copy-start(pred[1024]{0:T(1024)(128)(4,1)} %get-tuple-element.59) | copy-start | bytes 3076
Sparse Core Ops, SparseCore 0:
  9.0 41.9 all-gather.1
where the time goes:
time: 659 us; the launch traced here: 647 us
  waiting for transfers between devices  304 us (46%)
  local copies, waits for them, and re-layouts  199 us (30%)
  matrix products  77.3 us (12%)
  other arithmetic  36.6 us (6%)
  starting transfers between devices  15.2 us (2%)
  between operations  14.1 us (2%)
    all_to_all x1, waiting for transfers between devices, body(): lax.all_to_all(back_rows, ('dp', 'bag'), split_axis=1, concat_axis=1, til...  167 us
    all_to_all x1, waiting for transfers between devices, body(): lax.all_to_all(copies, ('dp', 'bag'), split_axis=1, concat_axis=1, tiled=...  97 us
    scatter x1, local copies, waits for them, and re-layouts, body(): jnp.full((send_slots,), pack_size, jnp.int32).at[recv_index]  60.3 us
    gather x2, local copies, waits for them, and re-layouts, body(): jnp.take(partial_low, slot_table, axis=0, mode='fill', fill_value=0)  46.7 us
    all_gather x1, waiting for transfers between devices, body(): pieces = lax.all_gather(home_tokens, 'bag', axis=1, tiled=True)  38.7 us
    gather x1, local copies, waits for them, and re-layouts, body(): packed = jnp.take(arrived, slot_source, axis=0, mode='fill', fill_value=0)  21.3 us
    dot_general x2, matrix products, attend(): jnp.einsum('hqk,khd->qhd', weights_soft, values, preferred_element_type=j...  19.9 us
    reshape x1, local copies, waits for them, and re-layouts, body(): arrived = arrived.reshape(send_slots, full_width)  19.5 us
  transfers between devices with their start and end apart: 3, of which 3 were waited for; matrix products, arithmetic and copies ran while one was open for 12% of the time, Pallas kernels for 0%

commit v1 on v0

v1 whole, which is shorter than its diff:
```python
import functools

import jax
import jax.numpy as jnp
from jax import lax
from jax.experimental import pallas as pl
from jax.experimental.pallas import tpu as pltpu
from jax.sharding import PartitionSpec as P

HD = 64
EPS = 1e-06
LOG2E = 1.4426950408889634


def head_norm(heads_in, gains):
    centre = jnp.mean(heads_in, axis=-1, keepdims=True)
    shifted = heads_in - centre
    spread = jnp.mean(shifted * shifted, axis=-1, keepdims=True)
    return shifted * lax.rsqrt(spread + EPS) * gains


def attention_kernel(q_ref, k_ref, v_ref, sq_ref, sk_ref, o_ref):
    def extend(x, sample, keep_low, fill):
        lane = lax.broadcasted_iota(jnp.int32, x.shape, 1)
        low = lane < HD
        hit = (lane % HD) == sample
        return jnp.where(low == keep_low, x, jnp.where(hit, fill, 0.0).astype(x.dtype))

    q, k, v = q_ref[...], k_ref[...], v_ref[...]
    lane_v = lax.broadcasted_iota(jnp.int32, v.shape, 1)
    outs = []
    for keep_low in (True, False):
        qx = extend(q, sq_ref[...], keep_low, 128.0)
        kx = extend(k, sk_ref[...], keep_low, 128.0)
        vx = jnp.where((lane_v < HD) == keep_low, v, jnp.ones_like(v))
        s = lax.dot_general(qx, kx, (((1,), (1,)), ((), ())), preferred_element_type=jnp.float32)
        m = jnp.max(s, axis=1, keepdims=True)
        p = jnp.exp2((s - m) * (LOG2E * HD ** -0.5)).astype(jnp.bfloat16)
        o = jnp.dot(p, vx, preferred_element_type=jnp.float32)
        outs.append(o / pltpu.roll(o, HD, 1))
    lane_o = lax.broadcasted_iota(jnp.int32, outs[0].shape, 1)
    o_ref[...] = jnp.where(lane_o < HD, outs[0], outs[1]).astype(o_ref.dtype)


def attention(q, k, v, sample_col):
    rows, width = q.shape
    bq = rows // 5
    return pl.pallas_call(
        attention_kernel,
        grid=(width // 128, rows // bq),
        in_specs=[
            pl.BlockSpec((bq, 128), lambda h, i: (i, h)),
            pl.BlockSpec((rows, 128), lambda h, i: (0, h)),
            pl.BlockSpec((rows, 128), lambda h, i: (0, h)),
            pl.BlockSpec((bq, 1), lambda h, i: (i, 0)),
            pl.BlockSpec((rows, 1), lambda h, i: (0, 0)),
        ],
        out_specs=pl.BlockSpec((bq, 128), lambda h, i: (i, h)),
        out_shape=jax.ShapeDtypeStruct((rows, width), jnp.bfloat16),
    )(q, k, v, sample_col, sample_col)


def plan_tables(row_plan, sample_lengths, modality, my_home, homes, resident, pack):
    cap = 2 * resident // homes
    dest = row_plan.reshape(homes, resident)
    bag = dest // pack
    slot = dest % pack
    bag_ids = jnp.arange(homes, dtype=jnp.int32)
    onehot = (bag[:, :, None] == bag_ids).astype(jnp.bfloat16)
    row_ids = jnp.arange(resident, dtype=jnp.int32)
    lower = (row_ids[:, None] > row_ids[None, :]).astype(jnp.bfloat16)
    ahead = jnp.einsum("mt,pta->pma", lower, onehot, preferred_element_type=jnp.float32)
    position = jnp.sum(ahead * onehot.astype(jnp.float32), axis=2).astype(jnp.int32)
    key = jnp.where(bag == my_home, position, -1)
    cap_ids = jnp.arange(cap, dtype=jnp.int32)
    slot_table = jnp.sum(
        jnp.where(key[:, None, :] == cap_ids[None, :, None], slot[:, None, :] + 1, 0), axis=2
    ).reshape(homes * cap) - 1
    own_bag = lax.dynamic_index_in_dim(bag, my_home, 0, keepdims=False)
    own_slot = lax.dynamic_index_in_dim(slot, my_home, 0, keepdims=False)
    own_index = own_bag * cap + lax.dynamic_index_in_dim(position, my_home, 0, keepdims=False)
    ends = jnp.cumsum(sample_lengths, axis=1)
    hits = (own_bag[:, None] == bag_ids[None, :])[:, :, None]
    row_ends = jnp.sum(jnp.where(hits, ends[None], 0), axis=1)
    row_mods = jnp.sum(jnp.where(hits, modality[None], 0), axis=1)
    row_sample = jnp.sum((own_slot[:, None] >= row_ends).astype(jnp.int32), axis=1)
    pick = row_sample[:, None] == jnp.arange(ends.shape[1], dtype=jnp.int32)[None, :]
    row_modality = jnp.sum(jnp.where(pick, row_mods, 0), axis=1)
    my_ends = jnp.sum(jnp.where((bag_ids == my_home)[:, None], ends, 0), axis=0)
    slot_ids = jnp.arange(pack, dtype=jnp.int32)
    sample_ids = jnp.sum((slot_ids[:, None] >= my_ends[None, :]).astype(jnp.int32), axis=1)
    return own_index, slot_table, row_modality, sample_ids


def pick_rows(left, right, rows):
    hot = (left == right).astype(jnp.bfloat16)
    return jnp.dot(hot, rows, preferred_element_type=jnp.float32).astype(jnp.bfloat16)


def body(
    home_tokens,
    mod_weight,
    qkv_weight,
    norm_gain,
    output_weight,
    row_plan,
    sample_lengths,
    modality,
):
    homes = lax.axis_size("dp")
    members = lax.axis_size("bag")
    my_home = lax.axis_index("dp")
    resident, part = home_tokens.shape
    pack = resident + resident // 4
    cap = 2 * resident // homes
    slots = cap * homes
    heads = part // HD
    own_index, slot_table, row_modality, sample_ids = plan_tables(
        row_plan, sample_lengths, modality, my_home, homes, resident, pack
    )
    slot_ids = jnp.arange(slots, dtype=jnp.int32)
    pack_ids = jnp.arange(pack, dtype=jnp.int32)
    weight_blocks = lax.all_to_all(
        output_weight.reshape(part, members, part), "bag", split_axis=1, concat_axis=0
    )
    tokens = lax.all_gather(home_tokens, "bag", axis=1, tiled=True)
    is_first = (row_modality == 0)[:, None]
    blank = jnp.zeros_like(tokens)
    projected = (
        jnp.dot(jnp.where(is_first, tokens, blank), mod_weight[0], preferred_element_type=jnp.float32)
        + jnp.dot(jnp.where(is_first, blank, tokens), mod_weight[1], preferred_element_type=jnp.float32)
    ).astype(jnp.bfloat16)
    outgoing = pick_rows(slot_ids[:, None], own_index[None, :], projected)
    arrived = lax.all_to_all(
        outgoing.reshape(homes, cap, part), "dp", split_axis=0, concat_axis=0, tiled=True
    ).reshape(slots, part)
    packed_part = pick_rows(pack_ids[:, None], slot_table[None, :], arrived)
    packed = lax.all_gather(packed_part, "bag", axis=1, tiled=True)
    stacked = jnp.einsum("pd,kdh->kph", packed, qkv_weight, preferred_element_type=jnp.float32)
    queries = head_norm(
        stacked[0].reshape(pack, heads, HD), norm_gain[0].reshape(heads, HD)
    ).astype(jnp.bfloat16).reshape(pack, part)
    keys = head_norm(
        stacked[1].reshape(pack, heads, HD), norm_gain[1].reshape(heads, HD)
    ).astype(jnp.bfloat16).reshape(pack, part)
    values = stacked[2].astype(jnp.bfloat16)
    attended = attention(queries, keys, values, sample_ids[:, None])
    back = pick_rows(slot_table[:, None], pack_ids[None, :], attended)
    returned = lax.all_to_all(
        back.reshape(homes, cap, part), "dp", split_axis=0, concat_axis=0, tiled=True
    ).reshape(slots, part)
    home_part = pick_rows(own_index[:, None], slot_ids[None, :], returned)
    home_rows = lax.all_gather(home_part, "bag", axis=0)
    partial = jnp.einsum(
        "gra,gab->grb", home_rows, weight_blocks.reshape(members, part, part), preferred_element_type=jnp.float32
    ).astype(jnp.bfloat16)
    return jnp.sum(partial.astype(jnp.float32), axis=0).astype(jnp.bfloat16)


def solution(mesh):
    in_specs = (
        P("dp", "bag"),
        P(None, None, "bag"),
        P(None, None, "bag"),
        P(None, "bag"),
        P("bag", None),
        P(),
        P(),
        P(),
    )
    return jax.shard_map(body, mesh=mesh, in_specs=in_specs, out_specs=P("dp", "bag"), check_vma=False)
```

time: 659 us -> 337 us (0.51)
  the two profiles are of different devices: /device:TPU:38 before, /device:TPU:1 now
where the time goes in v1:
time: 337 us
  waiting for transfers between devices  134 us (40%)
  blocking collectives  58.1 us (17%)
  matrix products  55.7 us (17%)
  local copies, waits for them, and re-layouts  26.9 us (8%)
  Pallas kernels  25.2 us (7%)
  starting transfers between devices  13.5 us (4%)
  between operations  13.4 us (4%)
  other arithmetic  10 us (3%)
    all_to_all x1, blocking collectives, body(): lax.all_to_all(output_weight.reshape(part, members, part), 'bag', split_a...  58.1 us
    all_gather x1, waiting for transfers between devices, body(): packed = lax.all_gather(packed_part, 'bag', axis=1, tiled=True)  45.3 us
    all_gather x1, waiting for transfers between devices, body(): tokens = lax.all_gather(home_tokens, 'bag', axis=1, tiled=True)  43.3 us
    pallas_call x1, Pallas kernels, attention(): pl.pallas_call(attention_kernel, grid=(width // 128, rows // bq), in_spec...  25.2 us
    dot_general x4, matrix products, pick_rows(): jnp.dot(hot, rows, preferred_element_type=jnp.float32).astype(jnp.bfloat16)  24.8 us
    all_to_all x1, waiting for transfers between devices, body(): lax.all_to_all(back.reshape(homes, cap, part), 'dp', split_axis=0, concat...  22.6 us
    all_to_all x1, waiting for transfers between devices, body(): lax.all_to_all(outgoing.reshape(homes, cap, part), 'dp', split_axis=0, co...  21.4 us
    dot_general x1, matrix products, body(): jnp.einsum('pd,kdh->kph', packed, qkv_weight, preferred_element_type=jnp....  13.5 us
  transfers between devices with their start and end apart: 5, of which 5 were waited for; matrix products, arithmetic and copies ran while one was open for 3% of the time, Pallas kernels for 0%

profile of v1, /device:TPU:1, one launch (start us, length us, event | category | flops | bytes accessed | tf_op | source)
XLA Modules:
  0.0 336.8 jit_solution(1832179356814620447)
XLA Ops:
  7.3 0.9 broadcast_remainder_fusion
  10.3 43.3 %all-gather.5.cloned.1.call-done = bf16[1024,3072]{1,0:T(8,128)(2,1)} async-done(((bf16[1024,384]{1,0:T(8,128)(2,1)}), bf16[1024,3072]{1,0:T(8,128)(2,1)}) %all-gather.5.cloned.1.call-update) | async-done | bytes 6291472 | tf_op jit(solution)/shard_map/all_gather | solution.py:126
  53.6 8.1 %fusion.6 = f32[1024,384]{1,0:T(8,128)} fusion(bf16[1024,3072]{1,0:T(8,128)(2,1)} %all-gather.5.cloned.1.call-done, pred[1024]{0:T(1024)(128)(4,1)S(1)} %broadcast_compare_fusion.1, bf16[2,3072,384]{2,1,0:T(8,128)(2,1)} %param.9), kind=kOutput, calls=%fused_computation.13 | convolution fusion | flops 2419064832 | bytes 10224640 | tf_op jit(solution)/shard_map/dot_general | solution.py:131
  61.7 10.8 %fusion.25 = bf16[2048,384]{1,0:T(8,128)(2,1)} fusion(s32[1024]{0:T(1024)S(1)} %bitcast.95, f32[1024,384]{1,0:T(8,128)} %fusion.6, bf16[2,3072,384]{2,1,0:T(8,128)(2,1)} %param.9, bf16[1024,3072]{1,0:T(8,128)(2,1)} %all-gather.5.cloned.1.call-done, pred[1024]{0:T(1024)(128)(4,1)S(1)} %broadcast_compare_fusion.1), kind=kOutput, calls=%fused_computation.30 | convolution fusion | flops 4033347584 | bytes 11801600 | tf_op jit(solution)/shard_map/dot_general | solution.py:97
  72.6 6.5 %all-to-all-start = ((bf16[16,128,384]{2,1,0:T(8,128)(2,1)}), bf16[16,128,384]{2,1,0:T(8,128)(2,1)S(1)}, u32[]{:S(2)}, u32[]{:S(2)}) async-start(bf16[16,128,384]{2,1,0:T(8,128)(2,1)} %bitcast.9), calls=%async_computation | async-start | bytes 3145728 | tf_op jit(solution)/shard_map/all_to_all | solution.py:134
  79.3 1.1 select_reduce_fusion
  80.4 21.4 %all-to-all-done = bf16[16,128,384]{2,1,0:T(8,128)(2,1)S(1)} async-done(((bf16[16,128,384]{2,1,0:T(8,128)(2,1)}), bf16[16,128,384]{2,1,0:T(8,128)(2,1)S(1)}, u32[]{:S(2)}, u32[]{:S(2)}) %all-to-all-start) | async-done | bytes 1572896 | tf_op jit(solution)/shard_map/all_to_all | solution.py:134
  101.8 3.9 %fusion.24 = bf16[1280,384]{1,0:T(8,128)(2,1)} fusion(bf16[2048,384]{1,0:T(8,128)(2,1)S(1)} %bitcast.89, s32[2048]{0:T(1024)S(1)} %add_bitcast_fusion), kind=kOutput, calls=%fused_computation.29 | convolution fusion | flops 2016378880 | bytes 2564096 | tf_op jit(solution)/shard_map/dot_general | solution.py:97
  106.0 1.1 broadcast_in_dim.119.sq_ref.sk_ref
  107.1 45.3 %all-gather.7.cloned.1.call-done = bf16[1280,3072]{1,0:T(8,128)(2,1)} async-done(((bf16[1280,384]{1,0:T(8,128)(2,1)}), bf16[1280,3072]{1,0:T(8,128)(2,1)}) %all-gather.7.cloned.1.call-update) | async-done | bytes 7864336 | tf_op jit(solution)/shard_map/all_gather | solution.py:138
  152.4 13.5 %fusion.14 = f32[3,1280,384]{2,1,0:T(8,128)S(1)} fusion(bf16[3,3072,384]{2,1,0:T(8,128)(2,1)} %param.10, bf16[1280,3072]{1,0:T(8,128)(2,1)} %all-gather.7.cloned.1.call-done), kind=kOutput, calls=%fused_computation.21 | convolution fusion | flops 9059696640 | bytes 20840448 | tf_op jit(solution)/shard_map/pd,kdh->kph/dot_general | solution.py:139
  165.9 2.4 fusion.62
  168.2 1.5 copy-done
  169.7 1.1 fusion.53.v_ref
  170.8 1.9 copy.43
  173.3 1.9 copy.45
  175.2 1.9 copy.46
  177.7 1.8 copy.48
  179.6 1.9 copy.44
  181.5 1.4 sub.53
  182.9 3.0 copy.47
  185.9 5.8 %fusion.34 = (bf16[1280,384]{1,0:T(8,128)(2,1)}, bf16[1280,384]{1,0:T(8,128)(2,1)}) fusion(f32[1280,384]{1,0:T(8,128)} %copy.48, f32[1280,384]{1,0:T(8,128)} %copy.47, f32[384]{0:T(512)S(1)} %get-tuple-element.7, f32[3,1280,384]{2,1,0:T(8,128)} %copy-done, f32[384]{0:T(512)S(1)} %get-tuple-element.8, f32[1280,384]{1,0:T(8,128)S(1)} %copy-done.1, ...), kind=kLoop, calls=%fused_computation.41 | loop fusion | flops 3932160 | bytes 13765632 | tf_op jit(solution)/shard_map/convert_element_type | solution.py:145
  191.7 25.2 %shard_map.82 = bf16[1280,384]{1,0:T(8,128)(2,1)} custom-call(bf16[1280,384]{1,0:T(8,128)(2,1)} %get-tuple-element.13.q_ref, bf16[1280,384]{1,0:T(8,128)(2,1)} %get-tuple-element.12.k_ref, bf16[1280,384]{1,0:T(8,128)(2,1)} %fusion.53.v_ref, s32[1280,1]{1,0:T(8,128)} %broadcast_in_dim.119.sq_ref.sk_ref, s32[1280,1]{1,0:T(8,128)} %broadcast_in_dim.119.sq_ref.sk_ref), custom_call_target="tpu_custom_call" | custom-call | tf_op jit(solution)/shard_map/pallas_call | solution.py:48
  216.9 5.3 %fusion.26 = bf16[2048,384]{1,0:T(8,128)(2,1)} fusion(bf16[1280,384]{1,0:T(8,128)(2,1)} %shard_map.82, s32[2048]{0:T(1024)S(1)} %add_bitcast_fusion), kind=kOutput, calls=%fused_computation.31 | convolution fusion | flops 2016673792 | bytes 2564096 | tf_op jit(solution)/shard_map/dot_general | solution.py:97
  222.1 6.5 %all-to-all-start.1 = ((bf16[16,128,384]{2,1,0:T(8,128)(2,1)}), bf16[16,128,384]{2,1,0:T(8,128)(2,1)S(1)}, u32[]{:S(2)}, u32[]{:S(2)}) async-start(bf16[16,128,384]{2,1,0:T(8,128)(2,1)} %bitcast.22), calls=%async_computation.1 | async-start | bytes 3145728 | tf_op jit(solution)/shard_map/all_to_all | solution.py:149
  228.9 22.6 %all-to-all-done.1 = bf16[16,128,384]{2,1,0:T(8,128)(2,1)S(1)} async-done(((bf16[16,128,384]{2,1,0:T(8,128)(2,1)}), bf16[16,128,384]{2,1,0:T(8,128)(2,1)S(1)}, u32[]{:S(2)}, u32[]{:S(2)}) %all-to-all-start.1) | async-done | bytes 1572896 | tf_op jit(solution)/shard_map/all_to_all | solution.py:149
  251.5 1.2 copy-done.3
  252.7 4.8 %fusion.42 = bf16[1024,384]{1,0:T(8,128)(2,1)} fusion(bf16[2048,384]{1,0:T(8,128)(2,1)} %bitcast.90, s32[1024]{0:T(1024)S(1)} %multiply_add_fusion.1), kind=kOutput, calls=%fused_computation.49 | convolution fusion | flops 1613103104 | bytes 2363392 | tf_op jit(solution)/shard_map/dot_general | solution.py:97
  257.5 2.5 copy.51
  260.0 3.0 copy.52
  263.0 58.1 %all_to_all.25 = bf16[1,384,8,384]{3,1,0,2:T(8,128)(2,1)} all-to-all(bf16[1,384,8,384]{3,1,0,2:T(8,128)(2,1)S(1)} %copy.52), channel_id=1, replica_groups=mesh['dp'=16,'bag'=8] {'bag'}, dimensions={2} | all-to-all | bytes 4718592 | tf_op jit(solution)/shard_map/all_to_all | solution.py:123
  321.8 8.5 %convert_reduce_fusion = bf16[1024,384]{1,0:T(8,128)(2,1)} fusion(bf16[8,1024,384]{2,1,0:T(8,128)(2,1)} %bitcast.96, bf16[1,384,8,384]{3,1,0,2:T(8,128)(2,1)} %all_to_all.25), kind=kOutput, calls=%fused_computation.12 | convolution fusion | flops 2421817344 | bytes 9437184 | tf_op jit(solution)/shard_map/gra,gab->grb/dot_general | solution.py:154
  (51 shorter events, 5.5 us)
Async XLA Ops:
  6.5 47.1 %all-gather.5.cloned.1.call-start = ((), (), s32[]{:S(2)}) async-start(), calls=%async_computation.3 | async-start | bytes 7077888 | tf_op jit(solution)/shard_map/all_gather | solution.py:126
  7.3 2.7 copy-start.5
  8.1 1.9 copy-start.6
  72.6 29.2 %all-to-all-start = ((bf16[16,128,384]{2,1,0:T(8,128)(2,1)}), bf16[16,128,384]{2,1,0:T(8,128)(2,1)S(1)}, u32[]{:S(2)}, u32[]{:S(2)}) async-start(bf16[16,128,384]{2,1,0:T(8,128)(2,1)} %bitcast.9), calls=%async_computation | async-start | bytes 3145728 | tf_op jit(solution)/shard_map/all_to_all | solution.py:134
  79.1 73.3 %all-gather.7.cloned.1.call-start = ((), (), s32[]{:S(2)}) async-start(), calls=%async_computation.4 | async-start | bytes 8847360 | tf_op jit(solution)/shard_map/all_gather | solution.py:138
  101.8 5.3 %copy-start.4 = (f32[2,384]{1,0:T(2,128)S(1)}, f32[2,384]{1,0:T(2,128)}, u32[]{:S(2)}) copy-start(f32[2,384]{1,0:T(2,128)} %param.11) | copy-start | bytes 9220
  165.9 3.9 %copy-start = (f32[3,1280,384]{2,1,0:T(8,128)}, f32[3,1280,384]{2,1,0:T(8,128)S(1)}, u32[]{:S(2)}) copy-start(f32[3,1280,384]{2,1,0:T(8,128)S(1)} %fusion.14) | copy-start | bytes 17694724
  182.9 3.0 copy-start.1
  222.1 29.4 %all-to-all-start.1 = ((bf16[16,128,384]{2,1,0:T(8,128)(2,1)}), bf16[16,128,384]{2,1,0:T(8,128)(2,1)S(1)}, u32[]{:S(2)}, u32[]{:S(2)}) async-start(bf16[16,128,384]{2,1,0:T(8,128)(2,1)} %bitcast.22), calls=%async_computation.1 | async-start | bytes 3145728 | tf_op jit(solution)/shard_map/all_to_all | solution.py:149
  228.7 93.1 %all-gather.9.cloned.1.call-start = ((), (), s32[]{:S(2)}) async-start(), calls=%async_computation.5 | async-start | bytes 7077888 | tf_op jit(solution)/shard_map/all_gather | solution.py:153
  251.5 1.2 copy-start.3
  252.7 4.8 %copy-start.2 = (bf16[384,3072]{1,0:T(8,128)(2,1)S(1)}, bf16[384,3072]{1,0:T(8,128)(2,1)}, u32[]{:S(2)}) copy-start(bf16[384,3072]{1,0:T(8,128)(2,1)} %param.12) | copy-start | bytes 7077892
Sparse Core Ops, SparseCore 0:
  9.0 44.5 all-gather.4
  105.9 46.4 all-gather.6
  257.6 64.1 all-gather.8

commit v2 on v1

v2 whole, which is shorter than its diff:
```python
import functools

import jax
import jax.numpy as jnp
from jax import lax
from jax.experimental import pallas as pl
from jax.experimental.pallas import tpu as pltpu
from jax.sharding import PartitionSpec as P

HD = 64
EPS = 1e-06
LOG2E = 1.4426950408889634


def plan_tables(row_plan, sample_lengths, modality, my_home, homes, resident, pack):
    cap = 2 * resident // homes
    dest = row_plan.reshape(homes, resident)
    bag = dest // pack
    slot = dest % pack
    bag_ids = jnp.arange(homes, dtype=jnp.int32)
    onehot = (bag[:, :, None] == bag_ids).astype(jnp.bfloat16)
    row_ids = jnp.arange(resident, dtype=jnp.int32)
    lower = (row_ids[:, None] > row_ids[None, :]).astype(jnp.bfloat16)
    ahead = jnp.einsum("mt,pta->pma", lower, onehot, preferred_element_type=jnp.float32)
    position = jnp.sum(ahead * onehot.astype(jnp.float32), axis=2).astype(jnp.int32)
    key = jnp.where(bag == my_home, position, -1)
    cap_ids = jnp.arange(cap, dtype=jnp.int32)
    slot_table = jnp.sum(
        jnp.where(key[:, None, :] == cap_ids[None, :, None], slot[:, None, :] + 1, 0), axis=2
    ).reshape(homes * cap) - 1
    own_bag = lax.dynamic_index_in_dim(bag, my_home, 0, keepdims=False)
    own_slot = lax.dynamic_index_in_dim(slot, my_home, 0, keepdims=False)
    own_index = own_bag * cap + lax.dynamic_index_in_dim(position, my_home, 0, keepdims=False)
    ends = jnp.cumsum(sample_lengths, axis=1)
    hits = (own_bag[:, None] == bag_ids[None, :])[:, :, None]
    row_ends = jnp.sum(jnp.where(hits, ends[None], 0), axis=1)
    row_mods = jnp.sum(jnp.where(hits, modality[None], 0), axis=1)
    row_sample = jnp.sum((own_slot[:, None] >= row_ends).astype(jnp.int32), axis=1)
    pick = row_sample[:, None] == jnp.arange(ends.shape[1], dtype=jnp.int32)[None, :]
    row_modality = jnp.sum(jnp.where(pick, row_mods, 0), axis=1)
    my_ends = jnp.sum(jnp.where((bag_ids == my_home)[:, None], ends, 0), axis=0)
    slot_ids = jnp.arange(pack, dtype=jnp.int32)
    sample_ids = jnp.sum((slot_ids[:, None] >= my_ends[None, :]).astype(jnp.int32), axis=1)
    return own_index, slot_table, row_modality, sample_ids


MESH = pl.DeviceIdType.MESH
LANES = 128


def remote(src, dst, send_sem, recv_sem, where):
    return pltpu.make_async_remote_copy(
        src_ref=src, dst_ref=dst, send_sem=send_sem, recv_sem=recv_sem, device_id=where, device_id_type=MESH
    )


class Ring:
    def __init__(self, first, buf, send_sems, recv_sems, places, on_ready):
        self.first, self.buf, self.send_sems, self.recv_sems = first, buf, send_sems, recv_sems
        self.near, self.far, self.twin = places
        self.on_ready = on_ready
        self.half = buf.shape[1] // 2
        self.sent, self.lands = [], {}

    def rows(self, half):
        return pl.ds(half * self.half, self.half)

    def view(self, k, lane, half):
        return self.buf.at[k, self.rows(half), pl.ds(lane * LANES, LANES)]

    def send(self, source, half, k, lane, where):
        copy = remote(source, self.view(k, lane, half), self.send_sems.at[len(self.sent)],
                      self.recv_sems.at[k, lane, half], where)
        copy.start()
        self.sent.append(copy)
        self.lands[k, lane, half] = copy

    def start(self):
        self.send(self.first(0), 0, 3, 0, self.near)
        self.send(self.first(1), 1, 1, 0, self.far)
        self.send(self.first(0), 0, 0, 1, self.twin)
        self.send(self.first(1), 1, 0, 1, self.twin)
        self.send(self.first(1), 1, 3, 0, self.near)
        self.send(self.first(0), 0, 1, 0, self.far)

    def forward(self, k, half):
        self.lands[k, 0, half].wait_recv()
        self.send(self.view(k, 0, half), half, k, 1, self.twin)

    def ready(self, k):
        for half in (0, 1):
            self.lands[k, 1, half].wait_recv()
        self.on_ready(k)

    def relay(self):
        for k, half, where in ((3, 0, self.near), (1, 1, self.far)):
            self.lands[k, 0, half].wait_recv()
            self.send(self.view(k, 0, half), half, 2, 0, where)
            self.send(self.view(k, 0, half), half, k, 1, self.twin)

    def own(self):
        self.ready(0)

    def beside(self):
        self.forward(3, 1)
        self.forward(1, 0)
        self.ready(3)
        self.ready(1)

    def across(self):
        self.forward(2, 0)
        self.forward(2, 1)
        self.ready(2)

    def finish(self):
        for copy in self.sent:
            copy.wait_send()


def loop(begin, end, step):
    def run(index, carry):
        step(index)
        return carry

    lax.fori_loop(begin, end, run, 0)


def head_scale(x, gain):
    low = lax.broadcasted_iota(jnp.int32, x.shape, 1) < HD

    def mean(t):
        left = jnp.sum(jnp.where(low, t, 0.0), axis=1, keepdims=True)
        right = jnp.sum(jnp.where(low, 0.0, t), axis=1, keepdims=True)
        return jnp.where(low, left, right) * (1.0 / HD)

    shifted = x - mean(x)
    return (shifted * lax.rsqrt(mean(shifted * shifted) + EPS) * gain).astype(jnp.bfloat16)


def extend(x, sample, keep_low):
    lane = lax.broadcasted_iota(jnp.int32, x.shape, 1)
    mark = jnp.where((lane % HD) == sample, 128.0, 0.0).astype(x.dtype)
    return jnp.where((lane < HD) == keep_low, x, mark)


def mega_kernel(
    homes_x, homes_y,
    tokens, modw, qkvw, outw, gain, own_row, table, cols,
    out,
    buf1, w1, acc1, proj, sbuf, abuf, buf2, w2, acc2, acc_pick, hots, kx, vx, att, back, buf3, w3, acc3,
    sem_w1, sem_w2, sem_w3s, sem_w3r, sem_own,
    s1, r1, s2, r2, s3, r3, sa, ra, sb, rb,
):
    homes = homes_x * homes_y
    me = lax.axis_index("dp")
    bag = lax.axis_index("bag")
    x, y = lax.div(me, homes_y), lax.rem(me, homes_y)
    z, core = lax.div(bag, 2), lax.rem(bag, 2)
    resident, part = tokens.shape
    pack = buf2.shape[2]
    cap = sbuf.shape[2]
    chunks = part // LANES
    f32, bf16 = jnp.float32, jnp.bfloat16

    def member(k, lane):
        return lax.rem(z + k, 4) * 2 + (core if lane == 0 else 1 - core)

    def home(turn, sign):
        step = lax.rem(turn * 5, homes)
        dx, dy = lax.div(step, homes_y), lax.rem(step, homes_y)
        if sign < 0:
            dx, dy = homes_x - dx, homes_y - dy
        return lax.rem(x + dx, homes_x) * homes_y + lax.rem(y + dy, homes_y)

    places = ({"bag": member(1, 0)}, {"bag": member(3, 0)}, {"bag": member(0, 1)})

    w1_loads, w2_loads = [], []
    for k in (0, 3, 1, 2):
        for lane in (0, 1):
            for m in range(2):
                w1_loads.append(pltpu.make_async_copy(
                    modw.at[m, member(k, lane)],
                    w1.at[:, k * 2 + lane, :, pl.ds(m * part, part)], sem_w1.at[len(w1_loads)]))
            for m in range(3):
                w2_loads.append(pltpu.make_async_copy(
                    qkvw.at[m, member(k, lane)],
                    w2.at[:, k * 2 + lane, :, pl.ds(m * part, part)], sem_w2.at[len(w2_loads)]))
    own_loads = [
        pltpu.make_async_copy(tokens.at[:, pl.ds(c * LANES, LANES)],
                              buf1.at[c, 0, :, pl.ds(0, LANES)], sem_own.at[c])
        for c in range(chunks)
    ]
    for load in own_loads + w1_loads:
        load.start()

    barrier = pltpu.get_barrier_semaphore()
    for turn in range(1, homes):
        pl.semaphore_signal(barrier, inc=1, device_id={"dp": home(turn, 1)}, device_id_type=MESH)
    for step in range(1, 8):
        pl.semaphore_signal(barrier, inc=1, device_id={"bag": lax.rem(bag + step, 8)}, device_id_type=MESH)
    pl.semaphore_wait(barrier, homes - 1 + 7)

    def spread(rows, hot):
        def one(turn):
            hots[pl.ds(0, rows), pl.ds(pl.multiple_of(turn * cap, cap), cap)] = hot(turn)

        loop(0, homes, one)

    def bag_hot(turn):
        ids = lax.broadcasted_iota(jnp.int32, (pack, cap), 0)
        return (ids == table[pl.ds(home(turn, -1), 1), :]).astype(bf16)

    def home_hot(turn):
        ids = lax.broadcasted_iota(jnp.int32, (resident, cap), 1) + home(turn, -1) * cap
        return (ids == cols[pl.ds(0, resident), 1:2]).astype(bf16)

    half1 = resident // 2

    def project(c, k):
        def tile(index):
            lanes = pl.ds(pl.multiple_of(index * 256, 256), 256)
            weight = w1[c, pl.ds(2 * k, 2), :, lanes].reshape(2 * LANES, 256)
            value = jnp.dot(buf1[c, k], weight, preferred_element_type=f32)
            if c == 0 and k == 0:
                acc1[:, lanes] = value
            else:
                acc1[:, lanes] += value

        loop(0, 2 * part // 256, tile)

    rings = [
        Ring(lambda half, c=c: tokens.at[pl.ds(half * half1, half1), pl.ds(c * LANES, LANES)],
             buf1.at[c], s1.at[c], r1.at[c], places, lambda k, c=c: project(c, k))
        for c in range(chunks)
    ]
    for ring in rings:
        ring.start()
    for load in own_loads + w1_loads:
        load.wait()
    for load in w2_loads:
        load.start()
    rings[0].own()
    rings[0].relay()
    rings[1].own()
    rings[1].relay()
    rings[0].beside()
    rings[2].own()
    rings[2].relay()
    rings[1].beside()
    rings[2].beside()
    spread(pack, bag_hot)
    for ring in rings:
        ring.across()
    is_first = cols[pl.ds(0, resident), 2:3] == 0
    proj[...] = jnp.where(is_first, acc1[:, :part], acc1[:, part:]).astype(bf16)

    def to_bag(c, turn):
        return remote(sbuf.at[c, turn], abuf.at[c, turn], sa.at[c, turn], ra.at[c, turn], {"dp": home(turn, 1)})

    def to_home(c, turn):
        return remote(sbuf.at[c, turn], back.at[c, turn], sb.at[c, turn], rb.at[c, turn], {"dp": home(turn, 1)})

    def stay(c, target, sem):
        return pltpu.make_async_copy(sbuf.at[c, 0], target.at[c, 0], sem.at[c, 0])

    group = 4

    def launch(c, index, copy, target, sem):
        for j in range(group):
            if j == 0:
                @pl.when(index == 0)
                def _():
                    stay(c, target, sem).start()

                @pl.when(index > 0)
                def _():
                    copy(c, index * group).start()
            else:
                copy(c, index * group + j).start()

    def fill(first, last):
        def some(index):
            hots = []
            for j in range(group):
                ids = lax.broadcasted_iota(jnp.int32, (cap, resident), 0) + home(index * group + j, 1) * cap
                hots.append((own_row[...] == ids).astype(bf16))
            block = jnp.dot(jnp.concatenate(hots, axis=0), proj[:, first * LANES:last * LANES],
                            preferred_element_type=f32).astype(bf16)
            for c in range(first, last):
                for j in range(group):
                    sbuf[c, index * group + j] = block[j * cap:(j + 1) * cap, (c - first) * LANES:(c - first + 1) * LANES]
                launch(c, index, to_bag, abuf, ra)

        loop(0, homes // group, some)

    fill(0, 1)
    fill(1, chunks)
    for ring in rings:
        ring.finish()

    def collect(c, source, sem, copy, rows):
        acc_pick[pl.ds(0, rows), :] = jnp.zeros((rows, LANES), f32)

        def take(index):
            values = []
            for j in range(group):
                turn = index * group + j
                if j == 0:
                    @pl.when(index == 0)
                    def _():
                        stay(c, source, sem).wait()

                    @pl.when(index > 0)
                    def _():
                        copy(c, turn).wait_recv()
                else:
                    copy(c, turn).wait_recv()
                values.append(source[c, turn])
            span = pl.ds(pl.multiple_of(index * group * cap, group * cap), group * cap)
            acc_pick[pl.ds(0, rows), :] += jnp.dot(
                hots[pl.ds(0, rows), span], jnp.concatenate(values, axis=0), preferred_element_type=f32)

        loop(0, homes // group, take)
        return acc_pick[pl.ds(0, rows), :].astype(bf16)

    half2 = pack // 2

    def qkv(c, k):
        def tile(index):
            rows = pl.ds(pl.multiple_of(index * half2, half2), half2)
            weight = w2[c, pl.ds(2 * k, 2)].reshape(2 * LANES, 3 * part)
            value = jnp.dot(buf2[c, k, rows, :], weight, preferred_element_type=f32)
            if c == 0 and k == 0:
                acc2[rows, :] = value
            else:
                acc2[rows, :] += value

        loop(0, 2, tile)

    rings = [
        Ring(lambda half, c=c: buf2.at[c, 0, pl.ds(half * half2, half2), pl.ds(0, LANES)],
             buf2.at[c], s2.at[c], r2.at[c], places, lambda k, c=c: qkv(c, k))
        for c in range(chunks)
    ]

    def pack_in(c):
        buf2[c, 0, :, 0:LANES] = collect(c, abuf, ra, to_bag, pack)
        rings[c].start()

    pack_in(0)
    pack_in(1)
    rings[0].relay()
    for load in w2_loads:
        load.wait()
    rings[0].own()
    pack_in(2)
    rings[1].own()
    rings[1].relay()
    rings[0].beside()
    rings[2].own()
    spread(resident, home_hot)
    rings[0].across()
    rings[2].relay()

    def columns(index):
        return outw.at[:, :, pl.ds(pl.multiple_of(index * part, part), part)]

    w3_own = pltpu.make_async_copy(columns(bag), w3.at[:, 0], sem_own.at[chunks])
    w3_own.start()
    w3_copies = []
    for k in range(4):
        for lane in range(2):
            if k or lane:
                target = lax.rem(z + 4 - k, 4) * 2 + (core if lane == 0 else 1 - core)
                index = k * 2 + lane
                copy = remote(columns(target), w3.at[:, index], sem_w3s.at[index], sem_w3r.at[index],
                              {"bag": target})
                copy.start()
                w3_copies.append(copy)

    rings[1].beside()
    rings[1].across()
    rings[2].beside()
    rings[2].across()
    for c in range(chunks):
        stay_turns = lambda turn, c=c: to_bag(c, turn).wait_send()
        loop(1, homes, stay_turns)
    for ring in rings:
        ring.finish()

    block_rows = pack // 5

    def prepare(pair):
        key = head_scale(acc2[:, pl.ds(part + pair * LANES, LANES)], gain[1:2, pl.ds(pair * LANES, LANES)])
        value = acc2[:, pl.ds(2 * part + pair * LANES, LANES)].astype(bf16)
        low = lax.broadcasted_iota(jnp.int32, value.shape, 1) < HD
        for head in range(2):
            kx[head] = extend(key, cols[pl.ds(0, pack), 3:4], head == 0)
            vx[head] = jnp.where(low == (head == 0), value, jnp.ones_like(value))

    def attend(pair, index):
        lanes = pl.ds(pair * LANES, LANES)
        rows = pl.ds(pl.multiple_of(index * block_rows, block_rows), block_rows)
        query = head_scale(acc2[rows, lanes], gain[0:1, lanes])
        results = []
        for head in range(2):
            qx = extend(query, cols[rows, 3:4], head == 0)
            s = lax.dot_general(qx, kx[head], (((1,), (1,)), ((), ())), preferred_element_type=f32)
            top = jnp.max(s, axis=1, keepdims=True)
            p = jnp.exp2((s - top) * (LOG2E * HD ** -0.5)).astype(bf16)
            o = jnp.dot(p, vx[head], preferred_element_type=f32)
            results.append(o / pltpu.roll(o, HD, 1))
        low_out = lax.broadcasted_iota(jnp.int32, results[0].shape, 1) < HD
        att[rows, :] = jnp.where(low_out, results[0], results[1]).astype(bf16)

    def send_back(c):
        def some(index):
            hots = []
            for j in range(group):
                ids = lax.broadcasted_iota(jnp.int32, (cap, pack), 1)
                begin = pl.multiple_of(home(index * group + j, 1) * cap, cap)
                hots.append((cols[pl.ds(begin, cap), 0:1] == ids).astype(bf16))
            block = jnp.dot(jnp.concatenate(hots, axis=0), att[...], preferred_element_type=f32).astype(bf16)
            for j in range(group):
                sbuf[c, index * group + j] = block[j * cap:(j + 1) * cap]
            launch(c, index, to_home, back, rb)

        loop(0, homes // group, some)

    def finish(c, k):
        weight = w3[c, pl.ds(2 * k, 2)].reshape(2 * LANES, part)
        value = jnp.dot(buf3[c, k], weight, preferred_element_type=f32)
        if c == 0 and k == 0:
            acc3[...] = value
        elif c == chunks - 1 and k == 2:
            out[...] = (acc3[...] + value).astype(bf16)
        else:
            acc3[...] += value

    rings = [
        Ring(lambda half, c=c: buf3.at[c, 0, pl.ds(half * half1, half1), pl.ds(0, LANES)],
             buf3.at[c], s3.at[c], r3.at[c], places, lambda k, c=c: finish(c, k))
        for c in range(chunks)
    ]

    def home_in(c):
        buf3[c, 0, :, 0:LANES] = collect(c, back, rb, to_home, resident)
        rings[c].start()

    prepare(0)
    loop(0, 5, lambda index: attend(0, index))
    send_back(0)
    prepare(1)
    loop(0, 5, lambda index: attend(1, index))
    send_back(1)
    home_in(0)
    prepare(2)
    loop(0, 3, lambda index: attend(2, index))
    rings[0].relay()
    home_in(1)
    loop(3, 5, lambda index: attend(2, index))
    send_back(2)
    w3_own.wait()
    for copy in w3_copies:
        copy.wait()
    rings[1].relay()
    rings[0].own()
    rings[0].beside()
    rings[1].own()
    rings[0].across()
    home_in(2)
    rings[1].beside()
    rings[1].across()
    rings[2].own()
    rings[2].relay()
    rings[2].beside()
    rings[2].across()
    for c in range(chunks):
        loop(1, homes, lambda turn, c=c: to_home(c, turn).wait_send())
    for ring in rings:
        ring.finish()


def body(
    home_tokens,
    mod_weight,
    qkv_weight,
    norm_gain,
    output_weight,
    row_plan,
    sample_lengths,
    modality,
):
    homes = lax.axis_size("dp")
    my_home = lax.axis_index("dp")
    resident, part = home_tokens.shape
    full = mod_weight.shape[1]
    pack = resident + resident // 4
    cap = 2 * resident // homes
    slots = cap * homes
    own_index, slot_table, row_modality, sample_ids = plan_tables(
        row_plan, sample_lengths, modality, my_home, homes, resident, pack
    )

    def pad(values):
        return jnp.pad(values, (0, slots - values.shape[0]))

    cols = jnp.stack([slot_table, pad(own_index), pad(row_modality), pad(sample_ids)], axis=1)
    bf16, f32 = jnp.bfloat16, jnp.float32
    any_spec = pl.BlockSpec(memory_space=pl.ANY)
    vmem = pl.BlockSpec(memory_space=pltpu.VMEM)
    dma = pltpu.SemaphoreType.DMA
    chunks = part // LANES
    members = full // part
    kernel = functools.partial(mega_kernel, 4, 4)
    ring_sems = [dma((chunks, 14)), dma((chunks, 4, 2, 2))]
    return pl.pallas_call(
        kernel,
        out_shape=jax.ShapeDtypeStruct((resident, part), bf16),
        in_specs=[any_spec] * 4 + [vmem] * 4,
        out_specs=vmem,
        scratch_shapes=[
            pltpu.VMEM((chunks, 4, resident, 2 * LANES), bf16),
            pltpu.VMEM((chunks, members, LANES, 2 * part), bf16),
            pltpu.VMEM((resident, 2 * part), f32),
            pltpu.VMEM((resident, part), bf16),
            pltpu.VMEM((chunks, homes, cap, LANES), bf16),
            pltpu.VMEM((chunks, homes, cap, LANES), bf16),
            pltpu.VMEM((chunks, 4, pack, 2 * LANES), bf16),
            pltpu.VMEM((chunks, members, LANES, 3 * part), bf16),
            pltpu.VMEM((pack, 3 * part), f32),
            pltpu.VMEM((pack, LANES), f32),
            pltpu.VMEM((pack, slots), bf16),
            pltpu.VMEM((2, pack, LANES), bf16),
            pltpu.VMEM((2, pack, LANES), bf16),
            pltpu.VMEM((pack, LANES), bf16),
            pltpu.VMEM((chunks, homes, cap, LANES), bf16),
            pltpu.VMEM((chunks, 4, resident, 2 * LANES), bf16),
            pltpu.VMEM((chunks, members, LANES, part), bf16),
            pltpu.VMEM((resident, part), f32),
            dma((16,)), dma((24,)), dma((8,)), dma((8,)), dma((chunks + 1,)),
            *ring_sems, *ring_sems, *ring_sems,
            *[dma((chunks, homes))] * 4,
        ],
        compiler_params=pltpu.CompilerParams(
            collective_id=0, has_side_effects=True, vmem_limit_bytes=67043328),
        name="mega",
    )(
        home_tokens,
        mod_weight.reshape(2, members, chunks, LANES, part),
        qkv_weight.reshape(3, members, chunks, LANES, part),
        output_weight.reshape(chunks, LANES, full),
        norm_gain, own_index[None, :], slot_table.reshape(homes, cap), cols,
    )


def solution(mesh):
    in_specs = (
        P("dp", "bag"),
        P(None, None, "bag"),
        P(None, None, "bag"),
        P(None, "bag"),
        P("bag", None),
        P(),
        P(),
        P(),
    )
    return jax.shard_map(body, mesh=mesh, in_specs=in_specs, out_specs=P("dp", "bag"), check_vma=False)
```

time: 337 us -> 179 us (0.53)
  Pallas kernels: 25.2 us -> 169 us
  waiting for transfers between devices: 134 us -> 0 us
  blocking collectives: 58.1 us -> 0 us
  matrix products: 55.7 us -> 0.84 us
  local copies, waits for them, and re-layouts: 26.9 us -> 3.53 us
  starting transfers between devices: 13.5 us -> 0 us
  between operations: 13.4 us -> 0.14 us
  other arithmetic: 10 us -> 5.35 us
    pallas_call x1, Pallas kernels: 25.2 us -> 169 us  [body(): pl.pallas_call(kernel, out_shape=jax.ShapeDtypeStruct((resident, part), b...]
    all_gather x3 -> x0, waiting for transfers between devices: 89.3 us -> none  [the longest x1 45.3 us: body(): packed = lax.all_gather(packed_part, 'bag', axis=1, tiled=True)]
    all_to_all x1 -> x0, blocking collectives: 58.1 us -> none  [body(): lax.all_to_all(output_weight.reshape(part, members, part), 'bag', split_a...]
    dot_general x7 -> x0, matrix products: 54.9 us -> none  [the longest x4 24.8 us: pick_rows(): jnp.dot(hot, rows, preferred_element_type=jnp.float32).astype(jnp.bfloat16)]
    all_to_all x2 -> x0, waiting for transfers between devices: 43.9 us -> none  [the longest x1 22.6 us: body(): lax.all_to_all(back.reshape(homes, cap, part), 'dp', split_axis=0, concat...]
    all_to_all x2 -> x0, starting transfers between devices: 13.1 us -> none  [the longest x1 6.53 us: body(): lax.all_to_all(back.reshape(homes, cap, part), 'dp', split_axis=0, concat...]
    sub x4 -> x0, local copies, waits for them, and re-layouts: 6.39 us -> none  [head_norm(): shifted = heads_in - centre]
    slice x4 -> x0, local copies, waits for them, and re-layouts: 6.14 us -> none  [the longest x2 4.24 us: body(): stacked[1].reshape(pack, heads, HD)]
  transfers between devices with their start and end apart: 5 -> 0, of which waited for: 5 -> 0; matrix products, arithmetic and copies ran while one was open for 3% -> 0% of each run, Pallas kernels for 0% -> 0%
where the time goes in v2:
time: 179 us
  Pallas kernels  169 us (94%)
  other arithmetic  5.35 us (3%)
  local copies, waits for them, and re-layouts  3.53 us (2%)
    pallas_call x1, Pallas kernels, body(): pl.pallas_call(kernel, out_shape=jax.ShapeDtypeStruct((resident, part), b...  169 us

profile of v2, /device:TPU:1, one launch (start us, length us, event | category | flops | bytes accessed | tf_op | source)
XLA Modules:
  0.0 178.6 jit_solution(17617169691415904355)
XLA Ops:
  0.0 0.7 reduce_window_sum.11
  0.7 0.1 select_reduce_fusion.4
  0.8 0.1 convert_reduce_fusion
  0.9 0.9 sign_compare_fusion
  1.8 0.9 broadcast_remainder_fusion
  2.8 0.8 fusion.9
  3.7 1.1 select_reduce_fusion
  4.8 0.0 copy-start
  4.8 0.6 multiply_add_fusion.1
  5.4 0.9 select_reduce_fusion.2
  6.3 0.0 copy-done
  6.4 1.4 copy.20.cols
  7.8 168.8 %mega.1 = bf16[1024,384]{1,0:T(8,128)(2,1)} custom-call(bf16[1024,384]{1,0:T(8,128)(2,1)} %tokens.1, bf16[2,8,3,128,384]{4,3,2,1,0:T(8,128)(2,1)} %bitcast.26, bf16[3,8,3,128,384]{4,3,2,1,0:T(8,128)(2,1)} %bitcast.25, bf16[3,128,3072]{2,1,0:T(8,128)(2,1)} %bitcast.27, f32[2,384]{1,0:T(2,128)} %gain.1, s32[1,1024]{1,0:T(1,128)} %get-tuple-element.7.own_row, ...), custom_call_target="tpu_custom_call" | custom-call | tf_op jit(solution)/shard_map/mega/pallas_call | solution.py:517
  176.5 2.1 %copy.22 = bf16[1024,384]{1,0:T(8,128)(2,1)} copy(bf16[1024,384]{1,0:T(8,128)(2,1)} %mega.1) | data formatting | bytes 1572864
  (16 shorter events, 0.2 us)
Async XLA Ops:
  4.8 1.6 copy-start

commit v3 on v2

--- a/solution.py
+++ b/solution.py
@@ -110,6 +110,8 @@
     def across(self):
         self.forward(2, 0)
         self.forward(2, 1)
+
+    def last(self):
         self.ready(2)
 
     def finish(self):
@@ -147,7 +149,7 @@
     homes_x, homes_y,
     tokens, modw, qkvw, outw, gain, own_row, table, cols,
     out,
-    buf1, w1, acc1, proj, sbuf, abuf, buf2, w2, acc2, acc_pick, hots, kx, vx, att, back, buf3, w3, acc3,
+    buf1, w1, acc1, proj, sbuf, abuf, buf2, w2, acc2, acc_pick, hots, qx, kx, vx, ahead, att, back, buf3, w3, acc3,
     sem_w1, sem_w2, sem_w3s, sem_w3r, sem_own,
     s1, r1, s2, r2, s3, r3, sa, ra, sb, rb,
 ):
@@ -200,11 +202,17 @@
         pl.semaphore_signal(barrier, inc=1, device_id={"bag": lax.rem(bag + step, 8)}, device_id_type=MESH)
     pl.semaphore_wait(barrier, homes - 1 + 7)
 
-    def spread(rows, hot):
-        def one(turn):
-            hots[pl.ds(0, rows), pl.ds(pl.multiple_of(turn * cap, cap), cap)] = hot(turn)
-
-        loop(0, homes, one)
+    def bag_block(index):
+        return hots.at[index]
+
+    def home_block(index):
+        return buf1.at[lax.div(index, 4), lax.rem(index, 4)]
+
+    def spread(block, hot):
+        def one(index):
+            block(index)[...] = jnp.concatenate([hot(2 * index), hot(2 * index + 1)], axis=1)
+
+        loop(0, homes // 2, one)
 
     def bag_hot(turn):
         ids = lax.broadcasted_iota(jnp.int32, (pack, cap), 0)
@@ -240,6 +248,7 @@
     for load in w2_loads:
         load.start()
     rings[0].own()
+    spread(bag_block, bag_hot)
     rings[0].relay()
     rings[1].own()
     rings[1].relay()
@@ -247,10 +256,13 @@
     rings[2].own()
     rings[2].relay()
     rings[1].beside()
+    rings[0].across()
     rings[2].beside()
-    spread(pack, bag_hot)
-    for ring in rings:
-        ring.across()
+    rings[1].across()
+    rings[0].last()
+    rings[1].last()
+    rings[2].across()
+    rings[2].last()
     is_first = cols[pl.ds(0, resident), 2:3] == 0
     proj[...] = jnp.where(is_first, acc1[:, :part], acc1[:, part:]).astype(bf16)
 
@@ -289,16 +301,37 @@
             for c in range(first, last):
                 for j in range(group):
                     sbuf[c, index * group + j] = block[j * cap:(j + 1) * cap, (c - first) * LANES:(c - first + 1) * LANES]
-                launch(c, index, to_bag, abuf, ra)
+                if c == first:
+                    launch(c, index, to_bag, abuf, ra)
 
         loop(0, homes // group, some)
 
+    def columns(index):
+        return outw.at[:, :, pl.ds(pl.multiple_of(index * part, part), part)]
+
+    w3_own = pltpu.make_async_copy(columns(bag), w3.at[:, 0], sem_own.at[chunks])
+    w3_copies = []
+
+    def share(k):
+        for lane in range(2):
+            if k or lane:
+                target = lax.rem(z + 4 - k, 4) * 2 + (core if lane == 0 else 1 - core)
+                index = k * 2 + lane
+                copy = remote(columns(target), w3.at[:, index], sem_w3s.at[index], sem_w3r.at[index],
+                              {"bag": target})
+                copy.start()
+                w3_copies.append(copy)
+
     fill(0, 1)
+    for k in (1, 3, 0):
+        share(k)
     fill(1, chunks)
+    for c in range(2, chunks):
+        loop(0, homes // group, lambda index, c=c: launch(c, index, to_bag, abuf, ra))
     for ring in rings:
         ring.finish()
 
-    def collect(c, source, sem, copy, rows):
+    def collect(c, source, sem, copy, rows, block):
         acc_pick[pl.ds(0, rows), :] = jnp.zeros((rows, LANES), f32)
 
         def take(index):
@@ -316,9 +349,9 @@
                 else:
                     copy(c, turn).wait_recv()
                 values.append(source[c, turn])
-            span = pl.ds(pl.multiple_of(index * group * cap, group * cap), group * cap)
+            hot = jnp.concatenate([block(2 * index)[...], block(2 * index + 1)[...]], axis=1)
             acc_pick[pl.ds(0, rows), :] += jnp.dot(
-                hots[pl.ds(0, rows), span], jnp.concatenate(values, axis=0), preferred_element_type=f32)
+                hot, jnp.concatenate(values, axis=0), preferred_element_type=f32)
 
         loop(0, homes // group, take)
         return acc_pick[pl.ds(0, rows), :].astype(bf16)
@@ -344,74 +377,68 @@
     ]
 
     def pack_in(c):
-        buf2[c, 0, :, 0:LANES] = collect(c, abuf, ra, to_bag, pack)
+        buf2[c, 0, :, 0:LANES] = collect(c, abuf, ra, to_bag, pack, bag_block)
         rings[c].start()
 
     pack_in(0)
+    spread(home_block, home_hot)
     pack_in(1)
     rings[0].relay()
     for load in w2_loads:
         load.wait()
     rings[0].own()
     pack_in(2)
+    rings[1].relay()
     rings[1].own()
-    rings[1].relay()
     rings[0].beside()
     rings[2].own()
-    spread(resident, home_hot)
+    rings[1].beside()
     rings[0].across()
     rings[2].relay()
-
-    def columns(index):
-        return outw.at[:, :, pl.ds(pl.multiple_of(index * part, part), part)]
-
-    w3_own = pltpu.make_async_copy(columns(bag), w3.at[:, 0], sem_own.at[chunks])
-    w3_own.start()
-    w3_copies = []
-    for k in range(4):
-        for lane in range(2):
-            if k or lane:
-                target = lax.rem(z + 4 - k, 4) * 2 + (core if lane == 0 else 1 - core)
-                index = k * 2 + lane
-                copy = remote(columns(target), w3.at[:, index], sem_w3s.at[index], sem_w3r.at[index],
-                              {"bag": target})
-                copy.start()
-                w3_copies.append(copy)
-
-    rings[1].beside()
+    rings[0].last()
+    rings[2].beside()
     rings[1].across()
-    rings[2].beside()
+    rings[1].last()
     rings[2].across()
+    rings[2].last()
     for c in range(chunks):
         stay_turns = lambda turn, c=c: to_bag(c, turn).wait_send()
         loop(1, homes, stay_turns)
     for ring in rings:
         ring.finish()
 
-    block_rows = pack // 5
+    blocks = 5
+    block_rows = pack // blocks
 
     def prepare(pair):
         key = head_scale(acc2[:, pl.ds(part + pair * LANES, LANES)], gain[1:2, pl.ds(pair * LANES, LANES)])
         value = acc2[:, pl.ds(2 * part + pair * LANES, LANES)].astype(bf16)
         low = lax.broadcasted_iota(jnp.int32, value.shape, 1) < HD
+        query = head_scale(acc2[:, pl.ds(pair * LANES, LANES)], gain[0:1, pl.ds(pair * LANES, LANES)])
         for head in range(2):
+            qx[head] = extend(query, cols[pl.ds(0, pack), 3:4], head == 0)
             kx[head] = extend(key, cols[pl.ds(0, pack), 3:4], head == 0)
             vx[head] = jnp.where(low == (head == 0), value, jnp.ones_like(value))
-
-    def attend(pair, index):
-        lanes = pl.ds(pair * LANES, LANES)
+        ahead[...] = score(0, 0)
+
+    def score(head, index):
         rows = pl.ds(pl.multiple_of(index * block_rows, block_rows), block_rows)
-        query = head_scale(acc2[rows, lanes], gain[0:1, lanes])
-        results = []
-        for head in range(2):
-            qx = extend(query, cols[rows, 3:4], head == 0)
-            s = lax.dot_general(qx, kx[head], (((1,), (1,)), ((), ())), preferred_element_type=f32)
-            top = jnp.max(s, axis=1, keepdims=True)
-            p = jnp.exp2((s - top) * (LOG2E * HD ** -0.5)).astype(bf16)
-            o = jnp.dot(p, vx[head], preferred_element_type=f32)
-            results.append(o / pltpu.roll(o, HD, 1))
-        low_out = lax.broadcasted_iota(jnp.int32, results[0].shape, 1) < HD
-        att[rows, :] = jnp.where(low_out, results[0], results[1]).astype(bf16)
+        return lax.dot_general(qx[head, rows, :], kx[head], (((1,), (1,)), ((), ())), preferred_element_type=f32)
+
+    def weigh(head, s):
+        top = jnp.max(s, axis=1, keepdims=True)
+        p = jnp.exp2((s - top) * (LOG2E * HD ** -0.5)).astype(bf16)
+        o = jnp.dot(p, vx[head], preferred_element_type=f32)
+        return o / pltpu.roll(o, HD, 1)
+
+    def attend(index):
+        rows = pl.ds(pl.multiple_of(index * block_rows, block_rows), block_rows)
+        odd_scores = score(1, index)
+        even = weigh(0, ahead[...])
+        ahead[...] = score(0, lax.rem(index + 1, blocks))
+        odd = weigh(1, odd_scores)
+        low = lax.broadcasted_iota(jnp.int32, even.shape, 1) < HD
+        att[rows, :] = jnp.where(low, even, odd).astype(bf16)
 
     def send_back(c):
         def some(index):
@@ -444,37 +471,43 @@
     ]
 
     def home_in(c):
-        buf3[c, 0, :, 0:LANES] = collect(c, back, rb, to_home, resident)
+        buf3[c, 0, :, 0:LANES] = collect(c, back, rb, to_home, resident, home_block)
         rings[c].start()
 
     prepare(0)
-    loop(0, 5, lambda index: attend(0, index))
+    loop(0, 1, attend)
+    w3_own.start()
+    share(2)
+    loop(1, blocks, attend)
     send_back(0)
     prepare(1)
-    loop(0, 5, lambda index: attend(1, index))
+    loop(0, blocks, attend)
     send_back(1)
     home_in(0)
     prepare(2)
-    loop(0, 3, lambda index: attend(2, index))
+    loop(0, 3, attend)
     rings[0].relay()
     home_in(1)
-    loop(3, 5, lambda index: attend(2, index))
+    loop(3, blocks, attend)
     send_back(2)
+    rings[1].relay()
     w3_own.wait()
     for copy in w3_copies:
         copy.wait()
-    rings[1].relay()
     rings[0].own()
     rings[0].beside()
+    rings[0].across()
     rings[1].own()
-    rings[0].across()
+    rings[0].last()
     home_in(2)
     rings[1].beside()
     rings[1].across()
     rings[2].own()
+    rings[1].last()
     rings[2].relay()
     rings[2].beside()
     rings[2].across()
+    rings[2].last()
     for c in range(chunks):
         loop(1, homes, lambda turn, c=c: to_home(c, turn).wait_send())
     for ring in rings:
@@ -530,9 +563,11 @@
             pltpu.VMEM((chunks, members, LANES, 3 * part), bf16),
             pltpu.VMEM((pack, 3 * part), f32),
             pltpu.VMEM((pack, LANES), f32),
-            pltpu.VMEM((pack, slots), bf16),
+            pltpu.VMEM((homes // 2, pack, 2 * LANES), bf16),
             pltpu.VMEM((2, pack, LANES), bf16),
             pltpu.VMEM((2, pack, LANES), bf16),
+            pltpu.VMEM((2, pack, LANES), bf16),
+            pltpu.VMEM((pack // 5, pack), f32),
             pltpu.VMEM((pack, LANES), bf16),
             pltpu.VMEM((chunks, homes, cap, LANES), bf16),
             pltpu.VMEM((chunks, 4, resident, 2 * LANES), bf16),

time: 179 us -> 163 us (0.911)
  Pallas kernels: 169 us -> 152 us
    pallas_call x1, Pallas kernels: 169 us -> 152 us  [body(): pl.pallas_call(kernel, out_shape=jax.ShapeDtypeStruct((resident, part), b...]
where the time goes in v3:
time: 163 us; the launch traced here: 162 us
  Pallas kernels  152 us (93%)
  other arithmetic  5.35 us (3%)
  local copies, waits for them, and re-layouts  3.53 us (2%)
    pallas_call x1, Pallas kernels, body(): pl.pallas_call(kernel, out_shape=jax.ShapeDtypeStruct((resident, part), b...  152 us

profile of v3, /device:TPU:1, one launch (start us, length us, event | category | flops | bytes accessed | tf_op | source)
XLA Modules:
  0.0 162.3 jit_solution(17056767988232801560)
XLA Ops:
  0.0 0.7 reduce_window_sum.11
  0.7 0.1 select_reduce_fusion.4
  0.8 0.1 convert_reduce_fusion
  0.9 0.9 sign_compare_fusion
  1.8 0.9 broadcast_remainder_fusion
  2.8 0.8 fusion.9
  3.7 1.1 select_reduce_fusion
  4.8 0.0 copy-start
  4.8 0.6 multiply_add_fusion.1
  5.4 0.9 select_reduce_fusion.2
  6.3 0.0 copy-done
  6.4 1.4 copy.20.cols
  7.8 152.4 %mega.1 = bf16[1024,384]{1,0:T(8,128)(2,1)} custom-call(bf16[1024,384]{1,0:T(8,128)(2,1)} %tokens.1, bf16[2,8,3,128,384]{4,3,2,1,0:T(8,128)(2,1)} %bitcast.26, bf16[3,8,3,128,384]{4,3,2,1,0:T(8,128)(2,1)} %bitcast.25, bf16[3,128,3072]{2,1,0:T(8,128)(2,1)} %bitcast.27, f32[2,384]{1,0:T(2,128)} %gain.1, s32[1,1024]{1,0:T(1,128)} %get-tuple-element.7.own_row, ...), custom_call_target="tpu_custom_call" | custom-call | tf_op jit(solution)/shard_map/mega/pallas_call | solution.py:550
  160.2 2.1 %copy.22 = bf16[1024,384]{1,0:T(8,128)(2,1)} copy(bf16[1024,384]{1,0:T(8,128)(2,1)} %mega.1) | data formatting | bytes 1572864
  (16 shorter events, 0.2 us)
Async XLA Ops:
  4.8 1.6 copy-start

commit v4 on v3

--- a/solution.py
+++ b/solution.py
@@ -10,38 +10,6 @@
 HD = 64
 EPS = 1e-06
 LOG2E = 1.4426950408889634
-
-
-def plan_tables(row_plan, sample_lengths, modality, my_home, homes, resident, pack):
-    cap = 2 * resident // homes
-    dest = row_plan.reshape(homes, resident)
-    bag = dest // pack
-    slot = dest % pack
-    bag_ids = jnp.arange(homes, dtype=jnp.int32)
-    onehot = (bag[:, :, None] == bag_ids).astype(jnp.bfloat16)
-    row_ids = jnp.arange(resident, dtype=jnp.int32)
-    lower = (row_ids[:, None] > row_ids[None, :]).astype(jnp.bfloat16)
-    ahead = jnp.einsum("mt,pta->pma", lower, onehot, preferred_element_type=jnp.float32)
-    position = jnp.sum(ahead * onehot.astype(jnp.float32), axis=2).astype(jnp.int32)
-    key = jnp.where(bag == my_home, position, -1)
-    cap_ids = jnp.arange(cap, dtype=jnp.int32)
-    slot_table = jnp.sum(
-        jnp.where(key[:, None, :] == cap_ids[None, :, None], slot[:, None, :] + 1, 0), axis=2
-    ).reshape(homes * cap) - 1
-    own_bag = lax.dynamic_index_in_dim(bag, my_home, 0, keepdims=False)
-    own_slot = lax.dynamic_index_in_dim(slot, my_home, 0, keepdims=False)
-    own_index = own_bag * cap + lax.dynamic_index_in_dim(position, my_home, 0, keepdims=False)
-    ends = jnp.cumsum(sample_lengths, axis=1)
-    hits = (own_bag[:, None] == bag_ids[None, :])[:, :, None]
-    row_ends = jnp.sum(jnp.where(hits, ends[None], 0), axis=1)
-    row_mods = jnp.sum(jnp.where(hits, modality[None], 0), axis=1)
-    row_sample = jnp.sum((own_slot[:, None] >= row_ends).astype(jnp.int32), axis=1)
-    pick = row_sample[:, None] == jnp.arange(ends.shape[1], dtype=jnp.int32)[None, :]
-    row_modality = jnp.sum(jnp.where(pick, row_mods, 0), axis=1)
-    my_ends = jnp.sum(jnp.where((bag_ids == my_home)[:, None], ends, 0), axis=0)
-    slot_ids = jnp.arange(pack, dtype=jnp.int32)
-    sample_ids = jnp.sum((slot_ids[:, None] >= my_ends[None, :]).astype(jnp.int32), axis=1)
-    return own_index, slot_table, row_modality, sample_ids
 
 
 MESH = pl.DeviceIdType.MESH
@@ -147,9 +115,9 @@
 
 def mega_kernel(
     homes_x, homes_y,
-    tokens, modw, qkvw, outw, gain, own_row, table, cols,
+    tokens, modw, qkvw, outw, gain, plan, lengths, modality,
     out,
-    buf1, w1, acc1, proj, sbuf, abuf, buf2, w2, acc2, acc_pick, hots, qx, kx, vx, ahead, att, back, buf3, w3, acc3,
+    own_row, table, cols, keys, buf1, w1, acc1, proj, sbuf, abuf, buf2, w2, acc2, acc_pick, hots, qx, kx, vx, ahead, att, back, buf3, w3, acc3,
     sem_w1, sem_w2, sem_w3s, sem_w3r, sem_own,
     s1, r1, s2, r2, s3, r3, sa, ra, sb, rb,
 ):
@@ -222,6 +190,73 @@
         ids = lax.broadcasted_iota(jnp.int32, (resident, cap), 1) + home(turn, -1) * cap
         return (ids == cols[pl.ds(0, resident), 1:2]).astype(bf16)
 
+    def split(rows):
+        bags = ((rows.astype(f32) + 0.5) * (1.0 / pack)).astype(jnp.int32)
+        return bags, rows - bags * pack
+
+    def ends_of(index):
+        ends = [lengths[index, 0]]
+        for sample in range(1, lengths.shape[1]):
+            ends.append(ends[-1] + lengths[index, sample])
+        return ends
+
+    def contract(left, right):
+        return lax.dot_general(left, right, (((1,), (1,)), ((), ())), preferred_element_type=f32)
+
+    def tables():
+        for piece in range(resident // 256):
+            before = lax.broadcasted_iota(jnp.int32, (resident, 256), 0)
+            after = lax.broadcasted_iota(jnp.int32, (resident, 256), 1) + piece * 256
+            hots[piece, 0:resident, :] = (before < after).astype(bf16)
+        bags, _ = split(plan[...])
+        own_bag, own_slot = split(plan[pl.ds(me, 1), :])
+        mine = bags == me
+        each = own_bag == lax.broadcasted_iota(jnp.int32, (homes, resident), 0)
+        both = jnp.concatenate([mine.astype(bf16), each.astype(bf16)], axis=0)
+        ranks = jnp.concatenate(
+            [jnp.dot(both, hots[piece, 0:resident, :], preferred_element_type=f32)
+             for piece in range(resident // 256)], axis=1)
+        keys[...] = jnp.where(mine, ranks[:homes].astype(jnp.int32), -1)
+        place = jnp.sum(jnp.where(each, ranks[homes:], 0.0), axis=0, keepdims=True).astype(jnp.int32)
+        own_row[...] = own_bag * cap + place
+        kind = jnp.zeros_like(own_bag)
+        for index in range(homes):
+            ends = ends_of(index)
+            value = jnp.full_like(own_bag, 0) + modality[index, len(ends) - 1]
+            for sample in range(len(ends) - 2, -1, -1):
+                value = jnp.where(own_slot < ends[sample], modality[index, sample], value)
+            kind = jnp.where(own_bag == index, value, kind)
+        line = lax.broadcasted_iota(jnp.int32, (8, resident), 0)
+        facts = jnp.where(line == 0, own_bag, jnp.where(line == 1, place, kind)).astype(bf16)
+
+        def same(index):
+            at = pl.multiple_of(index * 128, 128)
+            own = lax.broadcasted_iota(jnp.int32, (128, resident), 0) + at
+            hot = (own == lax.broadcasted_iota(jnp.int32, (128, resident), 1)).astype(bf16)
+            got = contract(hot, facts).astype(jnp.int32)
+            cols[pl.ds(at, 128), 1:2] = got[:, 0:1] * cap + got[:, 1:2]
+            cols[pl.ds(at, 128), 2:3] = got[:, 2:3]
+
+        loop(0, resident // 128, same)
+
+        def slots_of(index):
+            _, slot = split(plan[pl.ds(index, 1), :])
+            high = lax.shift_right_logical(slot, 8)
+            parts = jnp.where(line == 0, high, jnp.where(line == 1, slot - high * 256, 1)).astype(bf16)
+            hot = (lax.broadcasted_iota(jnp.int32, (cap, resident), 0) == keys[pl.ds(index, 1), :]).astype(bf16)
+            row = contract(parts, hot).astype(jnp.int32)
+            table[pl.ds(index, 1), :] = jnp.where(row[2:3] > 0, row[0:1] * 256 + row[1:2], -1)
+            col = contract(hot, parts).astype(jnp.int32)
+            at = pl.multiple_of(index * cap, cap)
+            cols[pl.ds(at, cap), 0:1] = jnp.where(col[:, 2:3] > 0, col[:, 0:1] * 256 + col[:, 1:2], -1)
+
+        loop(0, homes, slots_of)
+        here = lax.broadcasted_iota(jnp.int32, (pack, 1), 0)
+        sample = jnp.zeros_like(here)
+        for end in ends_of(me):
+            sample = sample + (here >= end).astype(jnp.int32)
+        cols[pl.ds(0, pack), 3:4] = sample
+
     half1 = resident // 2
 
     def project(c, k):
@@ -243,6 +278,7 @@
     ]
     for ring in rings:
         ring.start()
+    tables()
     for load in own_loads + w1_loads:
         load.wait()
     for load in w2_loads:
@@ -525,23 +561,15 @@
     modality,
 ):
     homes = lax.axis_size("dp")
-    my_home = lax.axis_index("dp")
     resident, part = home_tokens.shape
     full = mod_weight.shape[1]
     pack = resident + resident // 4
     cap = 2 * resident // homes
     slots = cap * homes
-    own_index, slot_table, row_modality, sample_ids = plan_tables(
-        row_plan, sample_lengths, modality, my_home, homes, resident, pack
-    )
-
-    def pad(values):
-        return jnp.pad(values, (0, slots - values.shape[0]))
-
-    cols = jnp.stack([slot_table, pad(own_index), pad(row_modality), pad(sample_ids)], axis=1)
     bf16, f32 = jnp.bfloat16, jnp.float32
     any_spec = pl.BlockSpec(memory_space=pl.ANY)
     vmem = pl.BlockSpec(memory_space=pltpu.VMEM)
+    smem = pl.BlockSpec(memory_space=pltpu.SMEM)
     dma = pltpu.SemaphoreType.DMA
     chunks = part // LANES
     members = full // part
@@ -550,9 +578,13 @@
     return pl.pallas_call(
         kernel,
         out_shape=jax.ShapeDtypeStruct((resident, part), bf16),
-        in_specs=[any_spec] * 4 + [vmem] * 4,
+        in_specs=[any_spec] * 4 + [vmem] * 2 + [smem] * 2,
         out_specs=vmem,
         scratch_shapes=[
+            pltpu.VMEM((1, resident), jnp.int32),
+            pltpu.VMEM((homes, cap), jnp.int32),
+            pltpu.VMEM((slots, 4), jnp.int32),
+            pltpu.VMEM((homes, resident), jnp.int32),
             pltpu.VMEM((chunks, 4, resident, 2 * LANES), bf16),
             pltpu.VMEM((chunks, members, LANES, 2 * part), bf16),
             pltpu.VMEM((resident, 2 * part), f32),
@@ -585,7 +617,7 @@
         mod_weight.reshape(2, members, chunks, LANES, part),
         qkv_weight.reshape(3, members, chunks, LANES, part),
         output_weight.reshape(chunks, LANES, full),
-        norm_gain, own_index[None, :], slot_table.reshape(homes, cap), cols,
+        norm_gain, row_plan.reshape(homes, resident), sample_lengths, modality,
     )
 
 

time: 163 us -> 159 us (0.975)
  other arithmetic: 5.35 us -> 0 us
  local copies, waits for them, and re-layouts: 3.53 us -> 6.27 us
    unnamed x3, local copies, waits for them, and re-layouts: 2.1 us -> 4.79 us
    reduce_sum x6 -> x0, other arithmetic: 2.17 us -> none  [the longest x1 1.07 us: plan_tables(): jnp.sum(jnp.where(key[:, None, :] == cap_ids[None, :, None], slot[:, None...]
where the time goes in v4:
time: 159 us; the launch traced here: 158 us
  Pallas kernels  152 us (96%)
  local copies, waits for them, and re-layouts  6.27 us (4%)
    pallas_call x1, Pallas kernels, body(): pl.pallas_call(kernel, out_shape=jax.ShapeDtypeStruct((resident, part), b...  152 us
    unnamed x3, local copies, waits for them, and re-layouts  4.79 us

profile of v4, /device:TPU:1, one launch (start us, length us, event | category | flops | bytes accessed | tf_op | source)
XLA Modules:
  0.0 158.5 jit_solution(13156355425334110147)
XLA Ops:
  0.0 1.3 copy.9.lengths
  1.3 1.4 copy.10.modality
  2.7 1.5 reshape.15.plan
  4.2 152.2 %mega.1 = bf16[1024,384]{1,0:T(8,128)(2,1)} custom-call(bf16[1024,384]{1,0:T(8,128)(2,1)} %tokens.1, bf16[2,8,3,128,384]{4,3,2,1,0:T(8,128)(2,1)} %bitcast.4, bf16[3,8,3,128,384]{4,3,2,1,0:T(8,128)(2,1)} %bitcast.3, bf16[3,128,3072]{2,1,0:T(8,128)(2,1)} %bitcast.5, f32[2,384]{1,0:T(2,128)} %gain.1, s32[16,1024]{1,0:T(8,128)} %reshape.15.plan, ...), custom_call_target="tpu_custom_call" | custom-call | tf_op jit(solution)/shard_map/mega/pallas_call | solution.py:578
  156.4 2.1 %copy.12 = bf16[1024,384]{1,0:T(8,128)(2,1)} copy(bf16[1024,384]{1,0:T(8,128)(2,1)} %mega.1) | data formatting | bytes 1572864

commit v5 on v4

--- a/solution.py
+++ b/solution.py
@@ -115,9 +115,9 @@
 
 def mega_kernel(
     homes_x, homes_y,
-    tokens, modw, qkvw, outw, gain, plan, lengths, modality,
+    tokens, modw, qkvw, outw, gain, raw_plan, lengths, modality,
     out,
-    own_row, table, cols, keys, buf1, w1, acc1, proj, sbuf, abuf, buf2, w2, acc2, acc_pick, hots, qx, kx, vx, ahead, att, back, buf3, w3, acc3,
+    own_row, table, cols, keys, plan, buf1, w1, acc1, proj, sbuf, abuf, buf2, w2, acc2, acc_pick, hots, qx, kx, vx, ahead, att, back, buf3, w3, acc3,
     sem_w1, sem_w2, sem_w3s, sem_w3r, sem_own,
     s1, r1, s2, r2, s3, r3, sa, ra, sb, rb,
 ):
@@ -195,9 +195,9 @@
         return bags, rows - bags * pack
 
     def ends_of(index):
-        ends = [lengths[index, 0]]
-        for sample in range(1, lengths.shape[1]):
-            ends.append(ends[-1] + lengths[index, sample])
+        ends = [lengths[0, index]]
+        for sample in range(1, lengths.shape[0]):
+            ends.append(ends[-1] + lengths[sample, index])
         return ends
 
     def contract(left, right):
@@ -208,6 +208,13 @@
             before = lax.broadcasted_iota(jnp.int32, (resident, 256), 0)
             after = lax.broadcasted_iota(jnp.int32, (resident, 256), 1) + piece * 256
             hots[piece, 0:resident, :] = (before < after).astype(bf16)
+        pieces = resident // LANES
+
+        def line_up(index):
+            plan[pl.ds(index, 1), :] = jnp.concatenate(
+                [raw_plan[pl.ds(index * pieces + piece, 1), :] for piece in range(pieces)], axis=1)
+
+        loop(0, homes, line_up)
         bags, _ = split(plan[...])
         own_bag, own_slot = split(plan[pl.ds(me, 1), :])
         mine = bags == me
@@ -222,9 +229,9 @@
         kind = jnp.zeros_like(own_bag)
         for index in range(homes):
             ends = ends_of(index)
-            value = jnp.full_like(own_bag, 0) + modality[index, len(ends) - 1]
+            value = jnp.full_like(own_bag, 0) + modality[len(ends) - 1, index]
             for sample in range(len(ends) - 2, -1, -1):
-                value = jnp.where(own_slot < ends[sample], modality[index, sample], value)
+                value = jnp.where(own_slot < ends[sample], modality[sample, index], value)
             kind = jnp.where(own_bag == index, value, kind)
         line = lax.broadcasted_iota(jnp.int32, (8, resident), 0)
         facts = jnp.where(line == 0, own_bag, jnp.where(line == 1, place, kind)).astype(bf16)
@@ -348,8 +355,8 @@
     w3_own = pltpu.make_async_copy(columns(bag), w3.at[:, 0], sem_own.at[chunks])
     w3_copies = []
 
-    def share(k):
-        for lane in range(2):
+    def share(*blocks):
+        for k, lane in blocks:
             if k or lane:
                 target = lax.rem(z + 4 - k, 4) * 2 + (core if lane == 0 else 1 - core)
                 index = k * 2 + lane
@@ -359,8 +366,7 @@
                 w3_copies.append(copy)
 
     fill(0, 1)
-    for k in (1, 3, 0):
-        share(k)
+    share((1, 0), (3, 0), (0, 1))
     fill(1, chunks)
     for c in range(2, chunks):
         loop(0, homes // group, lambda index, c=c: launch(c, index, to_bag, abuf, ra))
@@ -412,6 +418,14 @@
         for c in range(chunks)
     ]
 
+    def return_hot(turn):
+        ids = lax.broadcasted_iota(jnp.int32, (cap, pack), 1)
+        hot = (cols[pl.ds(pl.multiple_of(home(turn, 1) * cap, cap), cap), 0:1] == ids).astype(bf16)
+        begin = lax.rem(turn, 2) * (pack // 2)
+        for piece in range(pack // 256):
+            rows = pl.ds(pl.multiple_of(begin + piece * cap, cap), cap)
+            hots[lax.div(turn, 2), rows, :] = hot[:, piece * 256:(piece + 1) * 256]
+
     def pack_in(c):
         buf2[c, 0, :, 0:LANES] = collect(c, abuf, ra, to_bag, pack, bag_block)
         rings[c].start()
@@ -424,6 +438,7 @@
         load.wait()
     rings[0].own()
     pack_in(2)
+    loop(0, homes, return_hot)
     rings[1].relay()
     rings[1].own()
     rings[0].beside()
@@ -476,14 +491,18 @@
         low = lax.broadcasted_iota(jnp.int32, even.shape, 1) < HD
         att[rows, :] = jnp.where(low, even, odd).astype(bf16)
 
+    pieces = pack // 256
+
     def send_back(c):
         def some(index):
-            hots = []
-            for j in range(group):
-                ids = lax.broadcasted_iota(jnp.int32, (cap, pack), 1)
-                begin = pl.multiple_of(home(index * group + j, 1) * cap, cap)
-                hots.append((cols[pl.ds(begin, cap), 0:1] == ids).astype(bf16))
-            block = jnp.dot(jnp.concatenate(hots, axis=0), att[...], preferred_element_type=f32).astype(bf16)
+            total = None
+            for piece in range(pieces):
+                left = jnp.concatenate(
+                    [hots[2 * index + j // 2, pl.ds(((j % 2) * pieces + piece) * cap, cap), :] for j in range(group)],
+                    axis=0)
+                value = jnp.dot(left, att[pl.ds(piece * 256, 256), :], preferred_element_type=f32)
+                total = value if total is None else total + value
+            block = total.astype(bf16)
             for j in range(group):
                 sbuf[c, index * group + j] = block[j * cap:(j + 1) * cap]
             launch(c, index, to_home, back, rb)
@@ -513,7 +532,7 @@
     prepare(0)
     loop(0, 1, attend)
     w3_own.start()
-    share(2)
+    share((2, 0), (2, 1), (1, 1), (3, 1))
     loop(1, blocks, attend)
     send_back(0)
     prepare(1)
@@ -585,6 +604,7 @@
             pltpu.VMEM((homes, cap), jnp.int32),
             pltpu.VMEM((slots, 4), jnp.int32),
             pltpu.VMEM((homes, resident), jnp.int32),
+            pltpu.VMEM((homes, resident), jnp.int32),
             pltpu.VMEM((chunks, 4, resident, 2 * LANES), bf16),
             pltpu.VMEM((chunks, members, LANES, 2 * part), bf16),
             pltpu.VMEM((resident, 2 * part), f32),
@@ -617,7 +637,7 @@
         mod_weight.reshape(2, members, chunks, LANES, part),
         qkv_weight.reshape(3, members, chunks, LANES, part),
         output_weight.reshape(chunks, LANES, full),
-        norm_gain, row_plan.reshape(homes, resident), sample_lengths, modality,
+        norm_gain, row_plan.reshape(-1, LANES), sample_lengths.T, modality.T,
     )
 
 

time: 159 us -> 151 us (0.950)
  local copies, waits for them, and re-layouts: 6.27 us -> 2.09 us
  Pallas kernels: 152 us -> 148 us
    pallas_call x1, Pallas kernels: 152 us -> 148 us  [body(): pl.pallas_call(kernel, out_shape=jax.ShapeDtypeStruct((resident, part), b...]
    unnamed x3 -> x1, local copies, waits for them, and re-layouts: 4.79 us -> 2.09 us
where the time goes in v5:
time: 151 us; the launch traced here: 150 us
  Pallas kernels  148 us (98%)
  local copies, waits for them, and re-layouts  2.09 us (1%)
    pallas_call x1, Pallas kernels, body(): pl.pallas_call(kernel, out_shape=jax.ShapeDtypeStruct((resident, part), b...  148 us

profile of v5, /device:TPU:1, one launch (start us, length us, event | category | flops | bytes accessed | tf_op | source)
XLA Modules:
  0.0 150.3 jit_solution(6350996735481530006)
XLA Ops:
  0.0 148.2 %mega.1 = bf16[1024,384]{1,0:T(8,128)(2,1)} custom-call(bf16[1024,384]{1,0:T(8,128)(2,1)} %tokens.1, bf16[2,8,3,128,384]{4,3,2,1,0:T(8,128)(2,1)} %bitcast.7, bf16[3,8,3,128,384]{4,3,2,1,0:T(8,128)(2,1)} %bitcast.6, bf16[3,128,3072]{2,1,0:T(8,128)(2,1)} %bitcast.8, f32[2,384]{1,0:T(2,128)} %gain.1, s32[128,128]{1,0:T(8,128)} %bitcast.9, s32[4,16]{1,0:T(4,128)} %bitcast.10, ...), custom_call_target="tpu_custom_call" | custom-call | tf_op jit(solution)/shard_map/mega/pallas_call | solution.py:597
  148.3 2.1 %copy.10 = bf16[1024,384]{1,0:T(8,128)(2,1)} copy(bf16[1024,384]{1,0:T(8,128)(2,1)} %mega.1) | data formatting | bytes 1572864
